TPU v7x, 32 devices: a whole 2x2x4 slice. The times are simulated.
32 devices in a mesh: groups: 2 (over y), tile: 16 (over z, x, core).
Axes of the slice: x: 2, y: 2, z: 4, core: 2. Of those that a mesh axis runs over, the one named last changes fastest.
Arguments:
- sar_faces: bfloat16 [512, 8, 128], P(('groups', 'tile')), parts along dimension 0, may hold values from -6 to 6
- dest_owner: int32 [512, 1], P(('groups', 'tile')), parts along dimension 0, may hold values from 0 to 15; in each aligned block of 16 rows (0 to 15, 16 to 31, ...) at most 2 rows name the same one
- face_slot: int32 [512], P(('groups', 'tile')), parts along dimension 0, may hold values from 0 to 31
- valid_pixels: int32 [512], P(('groups', 'tile')), parts along dimension 0, may hold values from 1 to 8
- cloud_mask: int32 [32, 256], P(('groups', 'tile')), parts along dimension 0, may hold values 0 or 1
- time_index: int32 [32], P(('groups', 'tile')), parts along dimension 0, may hold values from 0 to 999
- clean_latent: bfloat16 [32, 256, 384], P(('groups', 'tile')), parts along dimension 0, may hold values from -6 to 6
- noise_latent: bfloat16 [32, 256, 384], P(('groups', 'tile')), parts along dimension 0, may hold values from -6 to 6
- encoder_first: bfloat16 [3, 8, 16, 48], replicated, may hold values from -0.875 to 0.875
- encoder_second: bfloat16 [3, 8, 48, 48], replicated, may hold values from -0.5 to 0.5
- conv_kernel: bfloat16 [9, 384, 384], replicated, may hold values from -0.109375 to 0.109375
- norm_gain: float32 [384], replicated, may hold values from 0.5 to 2
Outputs:
- grad_kernel: float32 [18, 384, 384], P('groups'), parts along dimension 0
- grad_gain: float32 [768], P('groups'), parts along dimension 0
- grad_first: float32 [6, 8, 16, 48], P('groups'), parts along dimension 0
- grad_second: float32 [6, 8, 48, 48], P('groups'), parts along dimension 0
There are 2 independent parts, one for each index of `groups`. A program takes and returns all parts, laid end to end along the dimension named above; an argument that names none is the same for every part. Nothing has to cross between parts.
Inputs may be any that keep to these rules, and one draw needn't show every extreme that they name: `dest_owner`: among each device's 16 faces, at most 2 name one tile owner.
All inputs are finite; a program needn't handle non-finite values. No bound on the sum of `cloud_mask` on one device may be relied on, other than what follows from the above.
Results may differ from a plain program's by a relative error of at most 0.0038.
Values may be sent and summed in bfloat16 or wider, within the bound.
A program may use at most 64 MiB of HBM per device.

v0:
```python
import jax
import jax.numpy as jnp
from jax import lax
from jax.sharding import PartitionSpec as P

MOST = 2
NSTEPS = 1000


highest = lax.Precision.HIGHEST
epsilon = 1e-06


def with_halo(block, sides, width):
    for axis, dim in sides:
        count = lax.axis_size(axis)
        forward = [(i, i + 1) for i in range(count - 1)]
        backward = [(target, source) for source, target in forward]
        low = lax.ppermute(
            lax.slice_in_dim(block, block.shape[dim] - width, None, axis=dim), axis, forward
        )
        high = lax.ppermute(lax.slice_in_dim(block, 0, width, axis=dim), axis, backward)
        block = jnp.concatenate([low, block, high], axis=dim)
    return block


def shift_line(values, offset):
    if offset == 0:
        return values
    zeros = jnp.zeros_like(values[:, : abs(offset)])
    if offset > 0:
        return jnp.concatenate([values[:, offset:], zeros], axis=1)
    return jnp.concatenate([zeros, values[:, :offset]], axis=1)


def taps_forward(inputs, weight, spread):
    summed = jnp.zeros(inputs.shape[:3] + (weight.shape[-1],), jnp.float32)
    for shift_tap in range(3):
        shifted = shift_line(inputs, (shift_tap - 1) * spread)
        summed = summed + jnp.einsum(
            "flgi,gio->flgo", shifted, weight[shift_tap], preferred_element_type=jnp.float32
        )
    return summed


def taps_weight_grad(inputs, cotangent, spread, exact):
    pieces = []
    for shift_tap in range(3):
        shifted = shift_line(inputs, (shift_tap - 1) * spread)
        if exact:
            pieces.append(
                jnp.einsum(
                    "flgi,flgo->gio", shifted.astype(jnp.float32), cotangent, precision=highest
                )
            )
        else:
            pieces.append(
                jnp.einsum("flgi,flgo->gio", shifted, cotangent, preferred_element_type=jnp.float32)
            )
    return jnp.stack(pieces)


def taps_input_grad(cotangent, weight, spread):
    summed = jnp.zeros(cotangent.shape[:3] + (weight.shape[2],), jnp.float32)
    for shift_tap in range(3):
        moved = jnp.einsum(
            "flgo,gio->flgi", cotangent, weight[shift_tap], preferred_element_type=jnp.float32
        )
        summed = summed + shift_line(moved, -(shift_tap - 1) * spread)
    return summed


def encoder_forward(sar_faces, first_w, second_w):
    face_count, length, channels_in = sar_faces.shape
    groups = first_w.shape[1]
    inputs = sar_faces.reshape(face_count, length, groups, -1)
    first_out = taps_forward(inputs, first_w, 1)
    hidden = jax.nn.silu(first_out).astype(jnp.bfloat16)
    second = taps_forward(hidden, second_w, 2)
    encoded = (
        (hidden.astype(jnp.float32) + second).reshape(face_count, length, -1).astype(jnp.bfloat16)
    )
    return (encoded, (inputs, first_out, hidden))


def encoder_backward(saved, grad_face, first_w, second_w):
    inputs, first_out, hidden = saved
    groups = first_w.shape[1]
    face_count, length, channels = grad_face.shape
    cotangent = grad_face.reshape(face_count, length, groups, -1)
    second_part = taps_weight_grad(hidden, cotangent, 2, False)
    grad_hidden = cotangent.astype(jnp.float32) + taps_input_grad(cotangent, second_w, 2)
    logistic = jax.nn.sigmoid(first_out)
    grad_first_out = grad_hidden * logistic * (1.0 + first_out * (1.0 - logistic))
    first_part = taps_weight_grad(inputs, grad_first_out, 1, True)
    return (first_part, second_part)


def convolve_forward(padded, kernel, rows, columns):
    channels = kernel.shape[-1]
    summed = jnp.zeros((rows * columns, channels), jnp.float32)
    for row_tap in range(3):
        for col_tap in range(3):
            window = padded[row_tap : row_tap + rows, col_tap : col_tap + columns].reshape(
                -1, channels
            )
            summed = summed + jnp.dot(
                window, kernel[3 * row_tap + col_tap], preferred_element_type=jnp.float32
            )
    return summed


def convolve_backward(padded_act, padded_grad, kernel, rows, columns):
    channels = kernel.shape[-1]
    incoming = padded_grad[1 : rows + 1, 1 : columns + 1].reshape(-1, channels)
    flows = jnp.zeros((rows * columns, channels), jnp.float32)
    kernels = []
    for row_tap in range(3):
        for col_tap in range(3):
            window = padded_act[row_tap : row_tap + rows, col_tap : col_tap + columns].reshape(
                -1, channels
            )
            kernels.append(
                lax.dot_general(
                    window, incoming, (((0,), (0,)), ((), ())), preferred_element_type=jnp.float32
                )
            )
            moved = padded_grad[
                2 - row_tap : 2 - row_tap + rows, 2 - col_tap : 2 - col_tap + columns
            ].reshape(-1, channels)
            flows = flows + lax.dot_general(
                moved,
                kernel[3 * row_tap + col_tap],
                (((1,), (1,)), ((), ())),
                preferred_element_type=jnp.float32,
            )
    return (flows, jnp.stack(kernels))


def norm_backward(flows, lifted, normed, inverse, gain):
    logistic = jax.nn.sigmoid(lifted)
    grad_lift = flows * logistic * (1.0 + lifted * (1.0 - logistic))
    gain_part = jnp.sum(grad_lift * normed, axis=0)
    grad_norm = grad_lift * gain
    grad_hsum = inverse * (
        grad_norm - normed * jnp.mean(grad_norm * normed, axis=-1, keepdims=True)
    )
    return (gain_part, grad_hsum)


def body(
    sar_faces,
    dest_owner,
    face_slot,
    valid_pixels,
    cloud_mask,
    time_index,
    clean_latent,
    noise_latent,
    encoder_first,
    encoder_second,
    conv_kernel,
    norm_gain,
):
    owners = lax.axis_size("tile")
    slot_total = owners * MOST
    face_count, length, channels_in = sar_faces.shape
    rows, columns, channels = clean_latent.shape
    tile_faces = rows * columns // length
    owner_list = dest_owner[:, 0]
    onehot = (owner_list[:, None] == jnp.arange(owners, dtype=jnp.int32)[None, :]).astype(jnp.int32)
    before = jnp.cumsum(onehot, axis=0) - onehot
    within = jnp.sum(before * onehot, axis=1)
    buffer_at = owner_list * MOST + within
    placed = (jnp.arange(slot_total, dtype=jnp.int32)[:, None] == buffer_at[None, :]).astype(
        jnp.int32
    )
    placer = placed.astype(jnp.bfloat16)
    labels = jnp.stack(
        [
            jnp.sum(placed * face_slot[None, :], axis=1),
            jnp.sum(placed * valid_pixels[None, :], axis=1),
        ],
        axis=-1,
    )
    labels = labels.reshape(owners, MOST, 2)
    packed = jnp.einsum(
        "sf,fjc->sjc", placer, sar_faces, preferred_element_type=jnp.float32
    ).astype(jnp.bfloat16)
    arrived, recv_labels = (
        lax.all_to_all(
            packed.reshape(owners, MOST, length, channels_in),
            "tile",
            split_axis=0,
            concat_axis=0,
            tiled=True,
        ),
        lax.all_to_all(labels, "tile", split_axis=0, concat_axis=0, tiled=True),
    )
    raw_slots = arrived.reshape(slot_total, length, channels_in)
    received, saved = encoder_forward(raw_slots, encoder_first, encoder_second)
    recv_labels = recv_labels.reshape(slot_total, 2)
    recv_slot = recv_labels[:, 0]
    recv_count = recv_labels[:, 1]
    validity = (jnp.arange(length, dtype=jnp.int32)[None, :] < recv_count[:, None]).astype(
        jnp.float32
    )
    selector = recv_slot[:, None] == jnp.arange(tile_faces, dtype=jnp.int32)[None, :]
    masked = received * validity[..., None].astype(jnp.bfloat16)
    summed = jnp.einsum(
        "sp,sjc->pjc", selector.astype(jnp.bfloat16), masked, preferred_element_type=jnp.float32
    )
    covered = jnp.einsum(
        "sp,sj->pj", selector.astype(jnp.float32), validity, precision=highest
    ).reshape(-1, 1)
    condition = summed.reshape(-1, channels) / (1.0 + covered)
    time_value = (time_index[0].astype(jnp.float32) + 0.5) / NSTEPS
    noise_flat = noise_latent.astype(jnp.float32).reshape(-1, channels)
    clean_flat = clean_latent.astype(jnp.float32).reshape(-1, channels)
    hsum = (1.0 - time_value) * noise_flat + time_value * clean_flat + condition
    inverse = lax.rsqrt(jnp.mean(hsum * hsum, axis=-1, keepdims=True) + epsilon)
    normed = hsum * inverse
    lifted = normed * norm_gain
    activated = jax.nn.silu(lifted).astype(jnp.bfloat16).reshape(rows, columns, channels)
    extended = with_halo(activated, (("tile", 0),), 1)
    padded = jnp.pad(extended, ((0, 0), (1, 1), (0, 0)))
    predicted = convolve_forward(padded, conv_kernel, rows, columns)
    pixel_weight = (1 + cloud_mask).astype(jnp.float32).reshape(-1, 1)
    grad_pred = (pixel_weight * (predicted - clean_flat + noise_flat) / (rows * columns)).astype(
        jnp.bfloat16
    )
    grad_rows = with_halo(grad_pred.reshape(rows, columns, channels), (("tile", 0),), 1)
    padded_grad = jnp.pad(grad_rows, ((0, 0), (1, 1), (0, 0)))
    flows, kernel_part = convolve_backward(padded, padded_grad, conv_kernel, rows, columns)
    gain_part, grad_hsum = norm_backward(flows, lifted, normed, inverse, norm_gain)
    scaled = (grad_hsum / (1.0 + covered)).reshape(tile_faces, length, channels)
    slot_grads = (jnp.take(scaled, recv_slot, axis=0) * validity[..., None]).astype(jnp.bfloat16)
    first_part, second_part = encoder_backward(saved, slot_grads, encoder_first, encoder_second)
    reduced = lax.psum((kernel_part, gain_part, first_part, second_part), "tile")
    return (reduced[0], reduced[1], reduced[2], reduced[3])


def solution(mesh):
    placed = (
        P(("groups", "tile"), None, None),
        P(("groups", "tile"), None),
        P(("groups", "tile")),
        P(("groups", "tile")),
        P(("groups", "tile"), None),
        P(("groups", "tile")),
        P(("groups", "tile"), None, None),
        P(("groups", "tile"), None, None),
        P(),
        P(),
        P(),
        P(),
    )
    return jax.shard_map(
        body,
        mesh=mesh,
        in_specs=placed,
        out_specs=(
            P("groups", None, None),
            P("groups"),
            P("groups", None, None, None),
            P("groups", None, None, None),
        ),
        check_vma=False,
    )
```

profile of v0, /device:TPU:0, one launch (start us, length us, event | category | flops | bytes accessed | tf_op | source)
XLA Modules:
  0.0 230.9 jit_solution(7680729361910062843)
XLA Ops:
  7.2 0.8 fusion.122
  8.0 0.8 select_reduce_fusion.2
  8.8 0.7 multiply_add_fusion
  9.5 0.8 select_reduce_fusion.1
  10.4 0.6 copy.47
  11.1 7.4 %all-to-all-start = ((s32[16,2,2]{1,2,0:T(2,128)}), s32[16,2,2]{1,2,0:T(2,128)S(1)}, u32[]{:S(2)}, u32[]{:S(2)}) async-start(s32[16,2,2]{1,2,0:T(2,128)} %copy.47), calls=%async_computation | async-start | bytes 32768 | tf_op jit(solution)/shard_map/all_to_all | solution.py:198
  19.1 0.7 add_convert_fusion
  20.0 0.7 copy.50
  20.7 4.2 %all-to-all-done = s32[16,2,2]{1,2,0:T(2,128)S(1)} async-done(((s32[16,2,2]{1,2,0:T(2,128)}), s32[16,2,2]{1,2,0:T(2,128)S(1)}, u32[]{:S(2)}, u32[]{:S(2)}) %all-to-all-start) | async-done | bytes 288 | tf_op jit(solution)/shard_map/all_to_all | solution.py:198
  24.9 3.5 %all-to-all-start.1 = ((bf16[16,2,8,128]{3,2,1,0:T(8,128)(2,1)}), bf16[16,2,8,128]{3,2,1,0:T(8,128)(2,1)S(1)}, u32[]{:S(2)}, u32[]{:S(2)}) async-start(bf16[16,2,8,128]{3,2,1,0:T(8,128)(2,1)} %copy.50), calls=%async_computation.1 | async-start | bytes 131072 | tf_op jit(solution)/shard_map/all_to_all | solution.py:191
  29.0 6.3 %all-to-all-done.1 = bf16[16,2,8,128]{3,2,1,0:T(8,128)(2,1)S(1)} async-done(((bf16[16,2,8,128]{3,2,1,0:T(8,128)(2,1)}), bf16[16,2,8,128]{3,2,1,0:T(8,128)(2,1)S(1)}, u32[]{:S(2)}, u32[]{:S(2)}) %all-to-all-start.1) | async-done | bytes 65568 | tf_op jit(solution)/shard_map/all_to_all | solution.py:191
  35.3 0.4 reshape_reshape.3
  35.7 0.6 copy.51
  36.3 1.1 fusion.111
  37.4 0.4 convolution_add_fusion.1
  37.8 1.4 multiply_convert_fusion
  40.0 1.1 copy.54
  41.2 2.3 convert_element_type.87
  43.5 1.0 broadcast_multiply_fusion
  44.7 1.4 multiply_reduce_fusion.2
  46.1 1.4 multiply_convert_fusion.1
  47.5 1.3 collective-permute-start.1
  48.8 3.0 %collective-permute-start = (bf16[1,256,384]{2,1,0:T(8,128)(2,1)S(1)}, bf16[1,256,384]{2,1,0:T(8,128)(2,1)S(1)}, u32[]{:S(2)}, u32[]{:S(2)}) collective-permute-start(bf16[1,256,384]{2,1,0:T(8,128)(2,1)S(1)} %multiply_convert_fusion.1), channel_id=1, source_target_pairs={{0,1},{1,2},{2,3},{3,4},{4,5},{5,6},{6,7},{7,8},{8,9},{9,10},{10,1... | collective-permute-start | bytes 589832 | tf_op jit(solution)/shard_map/ppermute | solution.py:19
  51.8 1.0 collective-permute-done
  55.3 0.3 fusion.27
  55.6 1.3 collective-permute-start.3
  56.9 5.4 %collective-permute-start.2 = (bf16[1,256,384]{2,1,0:T(8,128)(2,1)S(1)}, bf16[1,256,384]{2,1,0:T(8,128)(2,1)S(1)}, u32[]{:S(2)}, u32[]{:S(2)}) collective-permute-start(bf16[1,256,384]{2,1,0:T(8,128)(2,1)S(1)} %bitcast.323), channel_id=1, source_target_pairs={{0,1},{1,2},{2,3},{3,4},{4,5},{5,6},{6,7},{7,8},{8,9},{9,10},{10,1... | collective-permute-start | bytes 589832 | tf_op jit(solution)/shard_map/ppermute | solution.py:19
  66.4 1.0 copy-done.2
  67.4 0.3 convolution_add_fusion.8
  68.3 0.3 convolution_add_fusion.5
  68.6 0.5 multiply_reduce_fusion
  69.3 0.6 gather_fusion
  69.9 0.4 gather.7
  70.3 0.7 fusion.29
  71.0 0.3 convolution_bitcast_fusion.14
  71.3 0.3 convolution_bitcast_fusion.13
  72.6 0.8 copy-done.11
  73.4 0.6 fusion.7
  74.1 0.7 convolution_bitcast_fusion.15
  74.7 0.7 convolution_bitcast_fusion.17
  75.4 0.7 convolution_bitcast_fusion.16
  76.1 0.9 pad_maximum_fusion
  77.0 0.7 pad_maximum_fusion.1
  77.8 33.9 %psum.29 = f32[384]{0:T(512)} all-reduce(f32[384]{0:T(512)S(1)} %get-tuple-element.5), channel_id=1, replica_groups=mesh['groups'=2,'tile'=16] {'tile'}, use_global_device_ids=true, to_apply=%region_7.8 | all-reduce | flops 384 | bytes 3072 | tf_op jit(solution)/shard_map/psum | solution.py:239
  111.6 105.6 %all-reduce.11.cloned.1.call-done = (f32[9,384,384]{2,1,0:T(8,128)}, f32[3,8,16,48]{3,2,1,0:T(8,128)}, f32[3,8,48,48]{3,2,1,0:T(8,128)}) async-done(((f32[9,384,384]{2,1,0:T(8,128)}, f32[3,8,16,48]{3,2,1,0:T(8,128)}, f32[3,8,48,48]{3,2,1,0:T(8,128)}), (f32[9,384,384]{2,1,0:T(8,128)}, f32[3,8,16,48]{3,2,1,0:T(8,128)}, f32[3,8,48,48]{3,2,1,0:T(8,128)})) %all-reduce.11.cloned.1.call-update) | async-done | bytes 5603344 | tf_op jit(solution)/shard_map/psum | solution.py:239
  217.2 5.3 %copy.98 = f32[9,384,384]{2,1,0:T(8,128)} copy(f32[9,384,384]{2,1,0:T(8,128)} %get-tuple-element.21) | data formatting | bytes 10616832
  222.5 0.7 copy.99
  223.2 0.8 copy.100
  (79 shorter events, 10.1 us)
Async XLA Ops:
  7.2 12.6 %copy-start = (bf16[16,8,128]{2,1,0:T(8,128)(2,1)S(1)}, bf16[16,8,128]{2,1,0:T(8,128)(2,1)}, u32[]{:S(2)}) copy-start(bf16[16,8,128]{2,1,0:T(8,128)(2,1)} %param.12) | copy-start | bytes 98308
  7.2 30.2 %copy-start.9 = (bf16[3,8,16,48]{3,2,1,0:T(8,128)(2,1)S(1)}, bf16[3,8,16,48]{3,2,1,0:T(8,128)(2,1)}, u32[]{:S(2)}) copy-start(bf16[3,8,16,48]{3,2,1,0:T(8,128)(2,1)} %param.20) | copy-start | bytes 110596
  11.1 13.9 %all-to-all-start = ((s32[16,2,2]{1,2,0:T(2,128)}), s32[16,2,2]{1,2,0:T(2,128)S(1)}, u32[]{:S(2)}, u32[]{:S(2)}) async-start(s32[16,2,2]{1,2,0:T(2,128)} %copy.47), calls=%async_computation | async-start | bytes 32768 | tf_op jit(solution)/shard_map/all_to_all | solution.py:198
  24.9 10.4 %all-to-all-start.1 = ((bf16[16,2,8,128]{3,2,1,0:T(8,128)(2,1)}), bf16[16,2,8,128]{3,2,1,0:T(8,128)(2,1)S(1)}, u32[]{:S(2)}, u32[]{:S(2)}) async-start(bf16[16,2,8,128]{3,2,1,0:T(8,128)(2,1)} %copy.50), calls=%async_computation.1 | async-start | bytes 131072 | tf_op jit(solution)/shard_map/all_to_all | solution.py:191
  28.4 188.8 %all-reduce.11.cloned.1.call-start = ((), (), s32[]{:S(2)}) async-start(), calls=%async_computation.2 | async-start | bytes 12189696 | tf_op jit(solution)/shard_map/psum | solution.py:239
  37.8 1.4 copy-start.5
  39.7 6.3 %copy-start.10 = (f32[384]{0:T(512)S(1)}, f32[384]{0:T(512)}, u32[]{:S(2)}) copy-start(f32[384]{0:T(512)} %param.23) | copy-start | bytes 4612
  41.2 11.8 %copy-start.1 = (bf16[9,384,384]{2,1,0:T(8,128)(2,1)S(1)}, bf16[9,384,384]{2,1,0:T(8,128)(2,1)}, u32[]{:S(2)}) copy-start(bf16[9,384,384]{2,1,0:T(8,128)(2,1)} %param.22) | copy-start | bytes 7962628
  47.5 4.4 %collective-permute-start.1 = (bf16[1,256,384]{2,1,0:T(8,128)(2,1)S(1)}, bf16[1,256,384]{2,1,0:T(8,128)(2,1)S(1)}, u32[]{:S(2)}, u32[]{:S(2)}) collective-permute-start(bf16[1,256,384]{2,1,0:T(8,128)(2,1)S(1)} %multiply_convert_fusion.1), channel_id=1, source_target_pairs={{1,0},{2,1},{3,2},{4,3},{5,4},{6,5},{7,6},{8,7},{9,8},{10,9},{11,1... | collective-permute-start | bytes 589832 | tf_op jit(solution)/shard_map/ppermute | solution.py:22
  48.8 4.1 %collective-permute-start = (bf16[1,256,384]{2,1,0:T(8,128)(2,1)S(1)}, bf16[1,256,384]{2,1,0:T(8,128)(2,1)S(1)}, u32[]{:S(2)}, u32[]{:S(2)}) collective-permute-start(bf16[1,256,384]{2,1,0:T(8,128)(2,1)S(1)} %multiply_convert_fusion.1), channel_id=1, source_target_pairs={{0,1},{1,2},{2,3},{3,4},{4,5},{5,6},{6,7},{7,8},{8,9},{9,10},{10,1... | collective-permute-start | bytes 589832 | tf_op jit(solution)/shard_map/ppermute | solution.py:19
  54.1 1.1 copy-start.3
  54.1 1.1 copy-start.4
  55.6 9.4 %collective-permute-start.3 = (bf16[1,256,384]{2,1,0:T(8,128)(2,1)S(1)}, bf16[1,256,384]{2,1,0:T(8,128)(2,1)S(1)}, u32[]{:S(2)}, u32[]{:S(2)}) collective-permute-start(bf16[1,256,384]{2,1,0:T(8,128)(2,1)S(1)} %bitcast.322), channel_id=1, source_target_pairs={{1,0},{2,1},{3,2},{4,3},{5,4},{6,5},{7,6},{8,7},{9,8},{10,9},{11,1... | collective-permute-start | bytes 589832 | tf_op jit(solution)/shard_map/ppermute | solution.py:22
  56.9 8.1 %collective-permute-start.2 = (bf16[1,256,384]{2,1,0:T(8,128)(2,1)S(1)}, bf16[1,256,384]{2,1,0:T(8,128)(2,1)S(1)}, u32[]{:S(2)}, u32[]{:S(2)}) collective-permute-start(bf16[1,256,384]{2,1,0:T(8,128)(2,1)S(1)} %bitcast.323), channel_id=1, source_target_pairs={{0,1},{1,2},{2,3},{3,4},{4,5},{5,6},{6,7},{7,8},{8,9},{9,10},{10,1... | collective-permute-start | bytes 589832 | tf_op jit(solution)/shard_map/ppermute | solution.py:19
  65.0 2.4 %copy-start.2 = (f32[9,384,384]{2,1,0:T(8,128)}, f32[9,384,384]{2,1,0:T(8,128)S(1)}, u32[]{:S(2)}) copy-start(f32[9,384,384]{2,1,0:T(8,128)S(1)} %fusion.9) | copy-start | bytes 15925252
  70.3 1.6 copy-start.6
  72.2 1.2 copy-start.11
  217.2 5.3 %copy-start.8 = (f32[3,8,16,48]{3,2,1,0:T(8,128)S(1)}, f32[3,8,16,48]{3,2,1,0:T(8,128)}, u32[]{:S(2)}) copy-start(f32[3,8,16,48]{3,2,1,0:T(8,128)} %get-tuple-element.23) | copy-start | bytes 221188
  217.2 6.0 %copy-start.7 = (f32[3,8,48,48]{3,2,1,0:T(8,128)S(1)}, f32[3,8,48,48]{3,2,1,0:T(8,128)}, u32[]{:S(2)}) copy-start(f32[3,8,48,48]{3,2,1,0:T(8,128)} %get-tuple-element.24) | copy-start | bytes 663556
Sparse Core Ops, SparseCore 0:
  77.9 139.2 all-reduce.10
where the time goes:
time: 231 us
  waiting for transfers between devices  117 us (51%)
  blocking collectives  33.9 us (15%)
  starting transfers between devices  21.9 us (9%)
  matrix products  16.4 us (7%)
  local copies, waits for them, and re-layouts  15.9 us (7%)
  between operations  15.3 us (7%)
  other arithmetic  10.3 us (4%)
    psum x1, waiting for transfers between devices, body(): lax.psum((kernel_part, gain_part, first_part, second_part), 'tile')  106 us
    psum x1, blocking collectives, body(): lax.psum((kernel_part, gain_part, first_part, second_part), 'tile')  33.9 us
    unnamed x27, local copies, waits for them, and re-layouts  8.66 us
    ppermute x2, starting transfers between devices, with_halo(): lax.ppermute(lax.slice_in_dim(block, block.shape[dim] - width, None, axis...  8.42 us
    all_to_all x1, starting transfers between devices, body(): lax.all_to_all(labels, 'tile', split_axis=0, concat_axis=0, tiled=True)  7.36 us
    all_to_all x1, waiting for transfers between devices, body(): lax.all_to_all(packed.reshape(owners, MOST, length, channels_in), 'tile',...  6.29 us
  transfers between devices with their start and end apart: 7, of which 4 were waited for; matrix products, arithmetic and copies ran while one was open for 2% of the time, Pallas kernels for 0%

commit v1 on v0

--- a/solution.py
+++ b/solution.py
@@ -1,6 +1,8 @@
 import jax
 import jax.numpy as jnp
 from jax import lax
+from jax.experimental import pallas as pl
+from jax.experimental.pallas import tpu as pltpu
 from jax.sharding import PartitionSpec as P
 
 MOST = 2
@@ -146,6 +148,462 @@
         grad_norm - normed * jnp.mean(grad_norm * normed, axis=-1, keepdims=True)
     )
     return (gain_part, grad_hsum)
+
+
+MESH = pl.DeviceIdType.MESH
+VM = pltpu.VMEM
+
+
+def entry_barrier(me, count):
+    barrier = pltpu.get_barrier_semaphore()
+    for k in range(1, count):
+        pl.semaphore_signal(
+            barrier, inc=1, device_id={"tile": lax.rem(me + k, count)}, device_id_type=MESH
+        )
+    pl.semaphore_wait(barrier, count - 1)
+
+
+def exchange_kernel(count, x_ref, o_ref, send, recv, local):
+    me = lax.axis_index("tile")
+    entry_barrier(me, count)
+    own = pltpu.make_async_copy(x_ref.at[me], o_ref.at[me], local)
+    own.start()
+    copies = []
+    for k in range(1, count):
+        to = lax.rem(me + k, count)
+        copy = pltpu.make_async_remote_copy(
+            src_ref=x_ref.at[to],
+            dst_ref=o_ref.at[me],
+            send_sem=send.at[k - 1],
+            recv_sem=recv.at[k - 1],
+            device_id={"tile": to},
+            device_id_type=MESH,
+        )
+        copy.start()
+        copies.append(copy)
+    own.wait()
+    for copy in copies:
+        copy.wait()
+
+
+def exchange(packed):
+    count = packed.shape[0]
+    return pl.pallas_call(
+        lambda *refs: exchange_kernel(count, *refs),
+        out_shape=jax.ShapeDtypeStruct(packed.shape, packed.dtype),
+        in_specs=[pl.BlockSpec(memory_space=VM)],
+        out_specs=pl.BlockSpec(memory_space=VM),
+        scratch_shapes=[
+            pltpu.SemaphoreType.DMA((count - 1,)),
+            pltpu.SemaphoreType.DMA((count - 1,)),
+            pltpu.SemaphoreType.DMA,
+        ],
+        compiler_params=pltpu.CompilerParams(collective_id=0, has_side_effects=True),
+        name="exchange",
+    )(packed)
+
+
+class Gather:
+    def __init__(self, buf, send, recv):
+        self.buf, self.send_sem, self.recv_sem = buf, send, recv
+        self.me = lax.axis_index("tile")
+        self.core = lax.rem(self.me, 2)
+        self.x = lax.rem(self.me // 2, 2)
+        self.z = self.me // 4
+        self.x_peer = self.z * 4 + (1 - self.x) * 2 + self.core
+        self.sibling = self.z * 4 + self.x * 2 + (1 - self.core)
+
+    def copy(self, chunk, to, index):
+        return pltpu.make_async_remote_copy(
+            src_ref=self.buf.at[chunk],
+            dst_ref=self.buf.at[chunk],
+            send_sem=self.send_sem.at[index],
+            recv_sem=self.recv_sem.at[chunk],
+            device_id={"tile": to},
+            device_id_type=MESH,
+        )
+
+    def at(self, back, x, core):
+        return lax.rem(self.z + 4 - back, 4) * 4 + x * 2 + core
+
+    def start(self):
+        self.copy(self.me, self.x_peer, 3).start()
+        self.copy(self.me, self.sibling, 4).start()
+        for k in (1, 3, 2):
+            to = lax.rem(self.z + k, 4) * 4 + self.x * 2 + self.core
+            self.copy(self.me, to, k - 1).start()
+
+    def pass_z(self, back):
+        chunk = self.at(back, self.x, self.core)
+        self.copy(chunk, self.x_peer, 0).wait_recv()
+        self.copy(chunk, self.x_peer, 5 + 2 * (back - 1)).start()
+        self.copy(chunk, self.sibling, 6 + 2 * (back - 1)).start()
+
+    def pass_x(self, back):
+        chunk = self.at(back, 1 - self.x, self.core)
+        self.copy(chunk, self.sibling, 0).wait_recv()
+        self.copy(chunk, self.sibling, 11 + back).start()
+
+    def take(self, back):
+        for x in (self.x, 1 - self.x):
+            chunk = self.at(back, x, 1 - self.core)
+            self.copy(chunk, self.sibling, 0).wait_recv()
+
+    def drain(self):
+        for index in range(15):
+            self.copy(self.me, self.sibling, index).wait_send()
+
+
+def moved(values, offset, axis):
+    extent = values.shape[axis]
+    rolled = pltpu.roll(values, (-offset) % extent, axis)
+    place = lax.broadcasted_iota(jnp.int32, values.shape, axis)
+    return jnp.where(place == (extent - 1 if offset > 0 else 0), 0.0, rolled)
+
+
+def halo_copies(src, halo, send, recv, me):
+    up = pltpu.make_async_remote_copy(
+        src_ref=src,
+        dst_ref=halo.at[1],
+        send_sem=send.at[0],
+        recv_sem=recv.at[1],
+        device_id={"tile": jnp.maximum(me - 1, 0)},
+        device_id_type=MESH,
+    )
+    down = pltpu.make_async_remote_copy(
+        src_ref=src,
+        dst_ref=halo.at[0],
+        send_sem=send.at[1],
+        recv_sem=recv.at[0],
+        device_id={"tile": jnp.minimum(me + 1, 15)},
+        device_id_type=MESH,
+    )
+    return up, down
+
+
+def middle_kernel(
+    act_ref,
+    clean_ref,
+    noise_ref,
+    weight_ref,
+    kernel_ref,
+    flows_ref,
+    grad_ref,
+    gathered_ref,
+    halo_a,
+    halo_g,
+    gather_send,
+    gather_recv,
+    a_send,
+    a_recv,
+    g_send,
+    g_recv,
+):
+    me = lax.axis_index("tile")
+    last = 15
+    columns = act_ref.shape[0]
+    f32 = jnp.float32
+    entry_barrier(me, 16)
+    a_up, a_down = halo_copies(act_ref, halo_a, a_send, a_recv, me)
+    g_up, g_down = halo_copies(grad_ref, halo_g, g_send, g_recv, me)
+
+    @pl.when(me > 0)
+    def _():
+        a_up.start()
+
+    @pl.when(me < last)
+    def _():
+        a_down.start()
+
+    gathered_ref[me] = act_ref[...].T
+    gather = Gather(gathered_ref, gather_send, gather_recv)
+    gather.start()
+
+    @pl.when(me == 0)
+    def _():
+        halo_a[0] = jnp.zeros_like(halo_a[0])
+        halo_g[0] = jnp.zeros_like(halo_g[0])
+
+    @pl.when(me == last)
+    def _():
+        halo_a[1] = jnp.zeros_like(halo_a[1])
+        halo_g[1] = jnp.zeros_like(halo_g[1])
+
+    own = act_ref[...]
+    sums = [jnp.dot(own, kernel_ref[3 + d], preferred_element_type=f32) for d in range(3)]
+
+    @pl.when(me > 0)
+    def _():
+        a_down.wait_recv()
+
+    @pl.when(me < last)
+    def _():
+        a_up.wait_recv()
+
+    above, below = halo_a[0], halo_a[1]
+    sums = [
+        sums[d]
+        + jnp.dot(above, kernel_ref[d], preferred_element_type=f32)
+        + jnp.dot(below, kernel_ref[6 + d], preferred_element_type=f32)
+        for d in range(3)
+    ]
+    predicted = sums[1] + moved(sums[0], -1, 0) + moved(sums[2], 1, 0)
+    grad = (
+        weight_ref[...]
+        * (predicted - clean_ref[...].astype(f32) + noise_ref[...].astype(f32))
+        / columns
+    ).astype(jnp.bfloat16)
+    grad_ref[...] = grad
+
+    @pl.when(me > 0)
+    def _():
+        g_up.start()
+
+    @pl.when(me < last)
+    def _():
+        g_down.start()
+
+    def back(values, tap):
+        return lax.dot_general(
+            values, kernel_ref[tap], (((1,), (1,)), ((), ())), preferred_element_type=f32
+        )
+
+    sums = [back(grad, 3 + d) for d in range(3)]
+    for k in (1, 3, 2):
+        gather.pass_z(k)
+
+    @pl.when(me > 0)
+    def _():
+        g_down.wait_recv()
+
+    @pl.when(me < last)
+    def _():
+        g_up.wait_recv()
+
+    above, below = halo_g[0], halo_g[1]
+    sums = [sums[d] + back(below, d) + back(above, 6 + d) for d in range(3)]
+    flows_ref[...] = sums[1] + moved(sums[0], 1, 0) + moved(sums[2], -1, 0)
+    for k in (0, 1, 3, 2):
+        gather.pass_x(k)
+    for k in (0, 1, 3, 2):
+        gather.take(k)
+    gather.drain()
+
+    @pl.when(me > 0)
+    def _():
+        a_up.wait_send()
+        g_up.wait_send()
+
+    @pl.when(me < last)
+    def _():
+        a_down.wait_send()
+        g_down.wait_send()
+
+
+def middle(activated, clean, noise, pixel_weight, kernel):
+    pixels, channels = activated.shape
+    dma = pltpu.SemaphoreType.DMA
+    return pl.pallas_call(
+        middle_kernel,
+        out_shape=(
+            jax.ShapeDtypeStruct((pixels, channels), jnp.float32),
+            jax.ShapeDtypeStruct((pixels, channels), jnp.bfloat16),
+            jax.ShapeDtypeStruct((16, channels, pixels), jnp.bfloat16),
+        ),
+        in_specs=[pl.BlockSpec(memory_space=VM)] * 5,
+        out_specs=(pl.BlockSpec(memory_space=VM),) * 3,
+        scratch_shapes=[
+            VM((2, pixels, channels), jnp.bfloat16),
+            VM((2, pixels, channels), jnp.bfloat16),
+            dma((15,)),
+            dma((16,)),
+            dma((2,)),
+            dma((2,)),
+            dma((2,)),
+            dma((2,)),
+        ],
+        compiler_params=pltpu.CompilerParams(
+            collective_id=1, has_side_effects=True, vmem_limit_bytes=40 * 2**20
+        ),
+        name="middle",
+    )(activated, clean, noise, pixel_weight, kernel)
+
+
+def outer_kernel(
+    grad_ref, gathered_ref, result_ref, grads, shifted, gather_send, gather_recv
+):
+    me = lax.axis_index("tile")
+    channels, pixels = gathered_ref.shape[1:]
+    entry_barrier(me, 16)
+    grads[me] = grad_ref[...]
+    gather = Gather(grads, gather_send, gather_recv)
+    gather.start()
+    zeros = jnp.zeros((3, channels, pixels), jnp.bfloat16)
+    shifted[:, :, 0:pixels] = zeros
+    shifted[:, :, 17 * pixels : 18 * pixels] = zeros
+
+    def shift_chunk(chunk):
+        plain = gathered_ref[chunk]
+        wide = plain.astype(jnp.float32)
+        here = pl.ds(pl.multiple_of((chunk + 1) * pixels, pixels), pixels)
+        shifted[0, :, here] = moved(wide, -1, 1).astype(jnp.bfloat16)
+        shifted[1, :, here] = plain
+        shifted[2, :, here] = moved(wide, 1, 1).astype(jnp.bfloat16)
+
+    def shift_some(low, high):
+        def step(i, carry):
+            shift_chunk(i)
+            return carry
+
+        lax.fori_loop(low, high, step, 0)
+
+    def multiply(back):
+        base = lax.rem(gather.z + 4 - back, 4) * 4
+        right = grads[pl.ds(base, 4)].reshape(4 * pixels, channels)
+
+        def step(tap, carry):
+            start = pl.multiple_of((base + tap // 3) * pixels, pixels)
+            left = shifted[lax.rem(tap, 3), :, pl.ds(start, 4 * pixels)]
+            product = jnp.dot(left, right, preferred_element_type=jnp.float32)
+            if back == 0:
+                result_ref[tap] = product
+            else:
+                result_ref[tap] = result_ref[tap] + product
+            return carry
+
+        lax.fori_loop(0, 9, step, 0)
+
+    shift_some(0, 6)
+    gather.pass_x(0)
+    gather.pass_z(1)
+    shift_some(6, 11)
+    gather.pass_z(3)
+    shift_some(11, 16)
+    gather.pass_z(2)
+    gather.take(0)
+    multiply(0)
+    for k in (1, 3, 2):
+        gather.pass_x(k)
+        gather.take(k)
+        multiply(k)
+    gather.drain()
+
+
+def outer(grad, gathered):
+    pixels, channels = grad.shape
+    dma = pltpu.SemaphoreType.DMA
+    return pl.pallas_call(
+        outer_kernel,
+        out_shape=jax.ShapeDtypeStruct((9, channels, channels), jnp.float32),
+        in_specs=[pl.BlockSpec(memory_space=VM)] * 2,
+        out_specs=pl.BlockSpec(memory_space=VM),
+        scratch_shapes=[
+            VM((16, pixels, channels), jnp.bfloat16),
+            VM((3, channels, 18 * pixels), jnp.bfloat16),
+            dma((15,)),
+            dma((16,)),
+        ],
+        compiler_params=pltpu.CompilerParams(
+            collective_id=2, has_side_effects=True, vmem_limit_bytes=48 * 2**20
+        ),
+        cost_estimate=pl.CostEstimate(
+            flops=2 * 9 * 16 * pixels * channels * channels,
+            bytes_accessed=20 * 2**20,
+            transcendentals=0,
+        ),
+        name="outer",
+    )(grad, gathered)
+
+
+def body16(
+    sar_faces,
+    dest_owner,
+    face_slot,
+    valid_pixels,
+    cloud_mask,
+    time_index,
+    clean_latent,
+    noise_latent,
+    encoder_first,
+    encoder_second,
+    conv_kernel,
+    norm_gain,
+):
+    owners = lax.axis_size("tile")
+    slot_total = owners * MOST
+    face_count, length, channels_in = sar_faces.shape
+    rows, columns, channels = clean_latent.shape
+    tile_faces = rows * columns // length
+    owner_list = dest_owner[:, 0]
+    onehot = (owner_list[:, None] == jnp.arange(owners, dtype=jnp.int32)[None, :]).astype(jnp.int32)
+    before = jnp.cumsum(onehot, axis=0) - onehot
+    within = jnp.sum(before * onehot, axis=1)
+    buffer_at = owner_list * MOST + within
+    placed = (jnp.arange(slot_total, dtype=jnp.int32)[:, None] == buffer_at[None, :]).astype(
+        jnp.int32
+    )
+    placer = placed.astype(jnp.bfloat16)
+    labels = jnp.stack(
+        [
+            jnp.sum(placed * face_slot[None, :], axis=1),
+            jnp.sum(placed * valid_pixels[None, :], axis=1),
+        ],
+        axis=-1,
+    )
+    packed = jnp.einsum(
+        "sf,fjc->sjc", placer, sar_faces, preferred_element_type=jnp.float32
+    ).astype(jnp.bfloat16)
+    label_rows = jnp.pad(
+        labels.astype(jnp.bfloat16)[:, None, :],
+        ((0, 0), (0, length - 1), (0, channels_in - 2)),
+    )
+    arrived = exchange(
+        jnp.concatenate([packed, label_rows], axis=1).reshape(
+            owners, MOST * 2 * length, channels_in
+        )
+    ).reshape(slot_total, 2 * length, channels_in)
+    raw_slots = arrived[:, :length]
+    recv_labels = arrived[:, length, :2].astype(jnp.int32)
+    received, saved = encoder_forward(raw_slots, encoder_first, encoder_second)
+    recv_slot = recv_labels[:, 0]
+    recv_count = recv_labels[:, 1]
+    validity = (jnp.arange(length, dtype=jnp.int32)[None, :] < recv_count[:, None]).astype(
+        jnp.float32
+    )
+    selector = recv_slot[:, None] == jnp.arange(tile_faces, dtype=jnp.int32)[None, :]
+    masked = received * validity[..., None].astype(jnp.bfloat16)
+    summed = jnp.einsum(
+        "sp,sjc->pjc", selector.astype(jnp.bfloat16), masked, preferred_element_type=jnp.float32
+    )
+    covered = jnp.einsum(
+        "sp,sj->pj", selector.astype(jnp.float32), validity, precision=highest
+    ).reshape(-1, 1)
+    condition = summed.reshape(-1, channels) / (1.0 + covered)
+    time_value = (time_index[0].astype(jnp.float32) + 0.5) / NSTEPS
+    noise_flat = noise_latent.astype(jnp.float32).reshape(-1, channels)
+    clean_flat = clean_latent.astype(jnp.float32).reshape(-1, channels)
+    hsum = (1.0 - time_value) * noise_flat + time_value * clean_flat + condition
+    inverse = lax.rsqrt(jnp.mean(hsum * hsum, axis=-1, keepdims=True) + epsilon)
+    normed = hsum * inverse
+    lifted = normed * norm_gain
+    activated = jax.nn.silu(lifted).astype(jnp.bfloat16)
+    pixel_weight = (1 + cloud_mask).astype(jnp.float32).reshape(-1, 1)
+    flows, grad_pred, gathered = middle(
+        activated,
+        clean_latent.reshape(-1, channels),
+        noise_latent.reshape(-1, channels),
+        pixel_weight,
+        conv_kernel,
+    )
+    gain_part, grad_hsum = norm_backward(flows, lifted, normed, inverse, norm_gain)
+    scaled = (grad_hsum / (1.0 + covered)).reshape(tile_faces, length, channels)
+    slot_grads = (jnp.take(scaled, recv_slot, axis=0) * validity[..., None]).astype(jnp.bfloat16)
+    first_part, second_part = encoder_backward(saved, slot_grads, encoder_first, encoder_second)
+    parts = (gain_part, first_part, second_part)
+    grad_pred, parts = lax.optimization_barrier((grad_pred, parts))
+    reduced = lax.psum(parts, "tile")
+    grad_kernel = outer(grad_pred, gathered)
+    return (grad_kernel, reduced[0], reduced[1], reduced[2])
 
 
 def body(
@@ -256,7 +714,7 @@
         P(),
     )
     return jax.shard_map(
-        body,
+        body16 if mesh.shape["tile"] == 16 else body,
         mesh=mesh,
         in_specs=placed,
         out_specs=(

time: 231 us -> 194 us (0.84)
  waiting for transfers between devices: 117 us -> 14.5 us
  Pallas kernels: 0 us -> 94.4 us
  starting transfers between devices: 21.9 us -> 0.04 us
  matrix products: 16.4 us -> 11.8 us
    pallas_call x0 -> x3, Pallas kernels: none -> 94.4 us  [the longest x1 52.3 us: outer(): pl.pallas_call(outer_kernel, out_shape=jax.ShapeDtypeStruct((9, channels,...]
    psum x1, waiting for transfers between devices: 106 us -> 14.5 us  [body16(): reduced = lax.psum(parts, 'tile')]
    ppermute x4 -> x0, starting transfers between devices: 11 us -> none  [the longest x2 8.42 us: with_halo(): lax.ppermute(lax.slice_in_dim(block, block.shape[dim] - width, None, axis...]
    all_to_all x2 -> x0, starting transfers between devices: 10.9 us -> none  [the longest x1 7.36 us: body(): lax.all_to_all(labels, 'tile', split_axis=0, concat_axis=0, tiled=True)]
    all_to_all x2 -> x0, waiting for transfers between devices: 10.5 us -> none  [the longest x1 6.29 us: body(): lax.all_to_all(packed.reshape(owners, MOST, length, channels_in), 'tile',...]
    dot_general x30 -> x3, matrix products: 8.51 us -> 1.32 us  [the longest x1 0.94 us: body16(): jnp.einsum('sp,sjc->pjc', selector.astype(jnp.bfloat16), masked, preferre...]
    unnamed x27 -> x37, local copies, waits for them, and re-layouts: 8.66 us -> 9 us
  transfers between devices with their start and end apart: 7 -> 1, of which waited for: 4 -> 1; matrix products, arithmetic and copies ran while one was open for 2% -> 0% of each run, Pallas kernels for 0% -> 27%
where the time goes in v1:
time: 194 us
  Pallas kernels  94.4 us (49%)
  blocking collectives  34.2 us (18%)
  local copies, waits for them, and re-layouts  15.6 us (8%)
  between operations  15.1 us (8%)
  waiting for transfers between devices  14.5 us (7%)
  matrix products  11.8 us (6%)
  other arithmetic  8.3 us (4%)
    pallas_call x1, Pallas kernels, outer(): pl.pallas_call(outer_kernel, out_shape=jax.ShapeDtypeStruct((9, channels,...  52.3 us
    psum x1, blocking collectives, body16(): reduced = lax.psum(parts, 'tile')  34.2 us
    pallas_call x1, Pallas kernels, middle(): pl.pallas_call(middle_kernel, out_shape=(jax.ShapeDtypeStruct((pixels, ch...  31.4 us
    psum x1, waiting for transfers between devices, body16(): reduced = lax.psum(parts, 'tile')  14.5 us
    pallas_call x1, Pallas kernels, exchange(): pl.pallas_call(lambda *refs: exchange_kernel(count, *refs), out_shape=jax...  10.8 us
    unnamed x37, local copies, waits for them, and re-layouts  9 us
    dot_general x6, matrix products, taps_forward(): jnp.einsum('flgi,gio->flgo', shifted, weight[shift_tap], preferred_elemen...  5.31 us
  transfers between devices with their start and end apart: 1, of which 1 were waited for; matrix products, arithmetic and copies ran while one was open for 0% of the time, Pallas kernels for 27%

profile of v1, /device:TPU:0, one launch (start us, length us, event | category | flops | bytes accessed | tf_op | source)
XLA Modules:
  0.0 193.9 jit_solution(13425994008147029323)
XLA Ops:
  7.2 0.7 fusion.50
  8.0 0.8 select_reduce_fusion.2
  8.8 0.7 multiply_add_fusion
  9.5 0.8 select_reduce_fusion.1
  10.4 0.3 convolution_convert_fusion
  10.7 0.7 copy.41
  11.4 10.8 %exchange.1 = bf16[16,32,128]{2,1,0:T(8,128)(2,1)} custom-call(bf16[16,32,128]{2,1,0:T(8,128)(2,1)} %bitcast.153), custom_call_target="tpu_custom_call" | custom-call | tf_op jit(solution)/shard_map/exchange/pallas_call | solution.py:191
  22.1 0.9 slice.76
  23.0 0.8 slice.77
  24.6 0.7 convert_bitcast_fusion
  25.7 0.1 copy.52.weight_ref
  25.8 0.2 copy.67
  26.1 1.2 fusion.39
  27.3 1.1 convolution_add_fusion.1
  28.4 2.2 %multiply_convert_fusion = (bf16[32,8,8,48]{3,0,1,2:T(8,128)(2,1)S(1)}, f32[32,8,8,48]{3,0,1,2:T(8,128)}) fusion(f32[8,32,8,48]{3,1,2,0:T(8,128)S(1)} %convolution_add_fusion.1, bf16[3,8,16,48]{3,2,1,0:T(8,128)(2,1)} %param.20, bf16[32,8,8,16]{0,3,2,1:T(8,128)(2,1)S(1)} %bitcast.149), kind=kOutput, calls=%fused_computation.29 | convolution fusion | flops 3342336 | bytes 1900544 | tf_op jit(solution)/shard_map/flgi,gio->flgo/dot_general | solution.py:42
  30.6 0.3 fusion.28
  30.9 0.3 convolution_add_fusion.3
  31.2 0.2 copy-done.6
  31.4 0.3 fusion.8
  31.6 1.1 copy.47
  32.8 1.5 convert_element_type.98
  34.4 0.9 fusion.22
  35.3 1.3 multiply_reduce_fusion.2
  36.7 0.2 multiply_convert_fusion.1.act_ref
  36.9 31.4 %middle.1 = (f32[256,384]{1,0:T(8,128)S(1)}, bf16[256,384]{1,0:T(8,128)(2,1)S(1)}, bf16[16,384,256]{2,1,0:T(8,128)(2,1)S(1)}) custom-call(bf16[256,384]{1,0:T(8,128)(2,1)S(1)} %multiply_convert_fusion.1.act_ref, bf16[256,384]{1,0:T(8,128)(2,1)S(1)} %bitcast.145, bf16[256,384]{1,0:T(8,128)(2,1)S(1)} %bitcast.146, f32[256,1]{1,0:T(8,128)S(1)} %copy.52.weight_ref, ...), custom_call_target="tpu_custom_call" | custom-call | tf_op jit(solution)/shard_map/middle/pallas_call | solution.py:406
  68.2 1.7 copy-done.4
  69.9 0.4 multiply_reduce_fusion
  70.3 0.3 divide_bitcast_fusion
  70.6 0.6 gather_fusion
  71.2 0.4 gather.7
  71.6 0.7 fusion.11
  72.3 0.3 convolution_bitcast_fusion.5
  72.6 0.3 convolution_bitcast_fusion.4
  72.9 0.3 convolution_bitcast_fusion.3
  73.2 0.3 convolution_bitcast_fusion
  73.5 0.3 convolution_bitcast_fusion.2
  73.9 1.6 fusion.7
  75.6 0.7 convolution_bitcast_fusion.6
  76.3 0.7 convolution_bitcast_fusion.8
  77.0 0.7 convolution_bitcast_fusion.7
  77.7 0.9 pad_maximum_fusion
  78.6 0.7 pad_maximum_fusion.1
  79.3 52.3 %outer.1 = f32[9,384,384]{2,1,0:T(8,128)} custom-call(bf16[256,384]{1,0:T(8,128)(2,1)S(1)} %get-tuple-element.13.grad_ref, bf16[16,384,256]{2,1,0:T(8,128)(2,1)S(1)} %copy-done.5), custom_call_target="tpu_custom_call" | custom-call | flops 10871635968 | bytes 20971520 | tf_op jit(solution)/shard_map/outer/pallas_call | solution.py:495
  131.6 34.2 %psum.21 = f32[384]{0:T(512)} all-reduce(f32[384]{0:T(512)S(1)} %get-tuple-element.15), channel_id=1, replica_groups=mesh['groups'=2,'tile'=16] {'tile'}, use_global_device_ids=true, to_apply=%region_7.8 | all-reduce | flops 384 | bytes 3072 | tf_op jit(solution)/shard_map/psum | solution.py:604
  165.7 14.5 %all-reduce.10.cloned.1.call-done = (f32[3,8,16,48]{3,2,1,0:T(8,128)}, f32[3,8,48,48]{3,2,1,0:T(8,128)}) async-done(((f32[3,8,16,48]{3,2,1,0:T(8,128)}, f32[3,8,48,48]{3,2,1,0:T(8,128)}), (f32[3,8,16,48]{3,2,1,0:T(8,128)}, f32[3,8,48,48]{3,2,1,0:T(8,128)})) %all-reduce.10.cloned.1.call-update) | async-done | bytes 294928 | tf_op jit(solution)/shard_map/psum | solution.py:604
  180.2 5.3 %copy.99 = f32[9,384,384]{2,1,0:T(8,128)} copy(f32[9,384,384]{2,1,0:T(8,128)} %outer.1) | data formatting | bytes 10616832
  185.5 0.7 copy.100
  186.2 0.8 copy.101
  (52 shorter events, 1.0 us)
Async XLA Ops:
  7.2 3.2 %copy-start = (bf16[16,8,128]{2,1,0:T(8,128)(2,1)S(1)}, bf16[16,8,128]{2,1,0:T(8,128)(2,1)}, u32[]{:S(2)}) copy-start(bf16[16,8,128]{2,1,0:T(8,128)(2,1)} %param.12) | copy-start | bytes 98308
  7.2 173.0 %all-reduce.10.cloned.1.call-start = ((), (), s32[]{:S(2)}) async-start(), calls=%async_computation | async-start | bytes 1572864 | tf_op jit(solution)/shard_map/psum | solution.py:604
  26.0 4.5 %copy-start.8 = (bf16[32,8,128]{0,2,1:T(8,128)(2,1)}, bf16[32,8,128]{0,2,1:T(8,128)(2,1)S(1)}, u32[]{:S(2)}) copy-start(bf16[32,8,128]{0,2,1:T(8,128)(2,1)S(1)} %copy.67) | copy-start | bytes 196612
  26.1 4.5 %copy-start.10 = (bf16[3,8,48,48]{3,2,1,0:T(8,128)(2,1)S(1)}, bf16[3,8,48,48]{3,2,1,0:T(8,128)(2,1)}, u32[]{:S(2)}) copy-start(bf16[3,8,48,48]{3,2,1,0:T(8,128)(2,1)} %param.21) | copy-start | bytes 331780
  30.6 0.8 copy-start.6
  30.6 4.7 %copy-start.2 = (bf16[1,256,384]{2,1,0:T(8,128)(2,1)S(1)}, bf16[1,256,384]{2,1,0:T(8,128)(2,1)}, u32[]{:S(2)}) copy-start(bf16[1,256,384]{2,1,0:T(8,128)(2,1)} %param.18) | copy-start | bytes 589828
  30.6 4.7 %copy-start.3 = (bf16[1,256,384]{2,1,0:T(8,128)(2,1)S(1)}, bf16[1,256,384]{2,1,0:T(8,128)(2,1)}, u32[]{:S(2)}) copy-start(bf16[1,256,384]{2,1,0:T(8,128)(2,1)} %param.19) | copy-start | bytes 589828
  30.6 6.1 %copy-start.14 = (f32[384]{0:T(512)S(1)}, f32[384]{0:T(512)}, u32[]{:S(2)}) copy-start(f32[384]{0:T(512)} %param.23) | copy-start | bytes 4612
  30.6 6.2 %copy-start.1 = (bf16[9,384,384]{2,1,0:T(8,128)(2,1)S(1)}, bf16[9,384,384]{2,1,0:T(8,128)(2,1)}, u32[]{:S(2)}) copy-start(bf16[9,384,384]{2,1,0:T(8,128)(2,1)} %kernel_ref.1) | copy-start | bytes 7962628
  68.2 1.7 copy-start.4
  69.9 2.3 %copy-start.7 = (bf16[32,8,8,48]{3,0,1,2:T(8,128)(2,1)S(1)}, bf16[32,8,8,48]{3,0,1,2:T(8,128)(2,1)}, u32[]{:S(2)}) copy-start(bf16[32,8,8,48]{3,0,1,2:T(8,128)(2,1)} %copy-done.6) | copy-start | bytes 589828
  69.9 3.3 %copy-start.11 = (bf16[3,8,48,48]{3,2,1,0:T(8,128)(2,1)S(1)}, bf16[3,8,48,48]{3,2,1,0:T(8,128)(2,1)}, u32[]{:S(2)}) copy-start(bf16[3,8,48,48]{3,2,1,0:T(8,128)(2,1)} %param.21) | copy-start | bytes 331780
  72.2 1.7 copy-start.15
  73.8 1.8 copy-start.9
  73.9 5.4 %copy-start.5 = (bf16[16,384,256]{2,1,0:T(8,128)(2,1)S(1)}, bf16[16,384,256]{2,1,0:T(8,128)(2,1)}, u32[]{:S(2)}) copy-start(bf16[16,384,256]{2,1,0:T(8,128)(2,1)} %copy-done.4) | copy-start | bytes 9437188
  180.2 5.3 %copy-start.13 = (f32[3,8,16,48]{3,2,1,0:T(8,128)S(1)}, f32[3,8,16,48]{3,2,1,0:T(8,128)}, u32[]{:S(2)}) copy-start(f32[3,8,16,48]{3,2,1,0:T(8,128)} %get-tuple-element.41) | copy-start | bytes 221188
  180.2 6.0 %copy-start.12 = (f32[3,8,48,48]{3,2,1,0:T(8,128)S(1)}, f32[3,8,48,48]{3,2,1,0:T(8,128)}, u32[]{:S(2)}) copy-start(f32[3,8,48,48]{3,2,1,0:T(8,128)} %get-tuple-element.42) | copy-start | bytes 663556
Sparse Core Ops, SparseCore 0:
  79.4 100.7 all-reduce.9

commit v2 on v1

--- a/solution.py
+++ b/solution.py
@@ -430,89 +430,166 @@
 
 
 def outer_kernel(
-    grad_ref, gathered_ref, result_ref, grads, shifted, gather_send, gather_recv
+    grad_ref,
+    gathered_ref,
+    parts_ref,
+    result_ref,
+    total_ref,
+    grads,
+    shifted,
+    sums,
+    landed,
+    gather_send,
+    gather_recv,
+    half_send,
+    half_recv,
+    sum_send,
+    sum_recv,
 ):
     me = lax.axis_index("tile")
     channels, pixels = gathered_ref.shape[1:]
+    part = channels // 2
+    f32 = jnp.float32
     entry_barrier(me, 16)
     grads[me] = grad_ref[...]
     gather = Gather(grads, gather_send, gather_recv)
     gather.start()
-    zeros = jnp.zeros((3, channels, pixels), jnp.bfloat16)
-    shifted[:, :, 0:pixels] = zeros
-    shifted[:, :, 17 * pixels : 18 * pixels] = zeros
-
-    def shift_chunk(chunk):
-        plain = gathered_ref[chunk]
-        wide = plain.astype(jnp.float32)
-        here = pl.ds(pl.multiple_of((chunk + 1) * pixels, pixels), pixels)
-        shifted[0, :, here] = moved(wide, -1, 1).astype(jnp.bfloat16)
-        shifted[1, :, here] = plain
-        shifted[2, :, here] = moved(wide, 1, 1).astype(jnp.bfloat16)
+    core, z = gather.core, gather.z
+    mine = pl.ds(pl.multiple_of(core * part, part), part)
+    rows = parts_ref.shape[0] // 2
+    my_rows = pl.ds(pl.multiple_of(core * rows, 8), rows)
+    other_rows = pl.ds(pl.multiple_of((1 - core) * rows, 8), rows)
+    z_near = (z + 1 - 2 * lax.rem(z, 2)) * 4 + lax.rem(me, 4)
+    z_far = lax.rem(z + 2, 4) * 4 + lax.rem(me, 4)
+
+    def sum_copy(src, dst, stage, to):
+        return pltpu.make_async_remote_copy(
+            src_ref=src,
+            dst_ref=dst,
+            send_sem=sum_send.at[stage],
+            recv_sem=sum_recv.at[stage],
+            device_id={"tile": to},
+            device_id_type=MESH,
+        )
+
+    hops = [
+        sum_copy(parts_ref.at[other_rows], landed.at[0], 0, gather.sibling),
+        sum_copy(sums.at[0], landed.at[1], 1, gather.x_peer),
+        sum_copy(sums.at[1], landed.at[2], 2, z_near),
+        sum_copy(sums.at[2], landed.at[3], 3, z_far),
+        sum_copy(total_ref.at[my_rows], total_ref.at[my_rows], 4, gather.sibling),
+    ]
+    hops[0].start()
+
+    def add_hop(stage):
+        hops[stage].wait_recv()
+        held = parts_ref[my_rows, :] if stage == 0 else sums[stage - 1]
+        if stage < 3:
+            sums[stage] = held + landed[stage]
+        else:
+            total_ref[my_rows, :] = held + landed[stage]
+        hops[stage + 1].start()
+
+    zeros = jnp.zeros((3 * part, pixels), jnp.bfloat16)
+    shifted[:, 0:pixels] = zeros
+    shifted[:, 17 * pixels : 18 * pixels] = zeros
 
     def shift_some(low, high):
-        def step(i, carry):
-            shift_chunk(i)
+        def step(chunk, carry):
+            plain = gathered_ref[chunk, mine, :]
+            wide = plain.astype(f32)
+            here = pl.ds(pl.multiple_of((chunk + 1) * pixels, pixels), pixels)
+            shifted[0:part, here] = moved(wide, -1, 1).astype(jnp.bfloat16)
+            shifted[part : 2 * part, here] = plain
+            shifted[2 * part : 3 * part, here] = moved(wide, 1, 1).astype(jnp.bfloat16)
             return carry
 
         lax.fori_loop(low, high, step, 0)
 
-    def multiply(back):
-        base = lax.rem(gather.z + 4 - back, 4) * 4
+    def half_copy(row):
+        return pltpu.make_async_remote_copy(
+            src_ref=result_ref.at[pl.ds(3 * row, 3), mine],
+            dst_ref=result_ref.at[pl.ds(3 * row, 3), mine],
+            send_sem=half_send.at[row],
+            recv_sem=half_recv.at[row],
+            device_id={"tile": gather.sibling},
+            device_id_type=MESH,
+        )
+
+    def multiply(back, order):
+        base = lax.rem(z + 4 - back, 4) * 4
         right = grads[pl.ds(base, 4)].reshape(4 * pixels, channels)
 
-        def step(tap, carry):
-            start = pl.multiple_of((base + tap // 3) * pixels, pixels)
-            left = shifted[lax.rem(tap, 3), :, pl.ds(start, 4 * pixels)]
-            product = jnp.dot(left, right, preferred_element_type=jnp.float32)
-            if back == 0:
-                result_ref[tap] = product
-            else:
-                result_ref[tap] = result_ref[tap] + product
+        def step(row, carry):
+            start = pl.multiple_of((base + row) * pixels, pixels)
+            left = shifted[:, pl.ds(start, 4 * pixels)]
+            product = jnp.dot(left, right, preferred_element_type=f32)
+            for d in range(3):
+                piece = product[d * part : (d + 1) * part]
+                if order == 0:
+                    result_ref[3 * row + d, mine, :] = piece
+                else:
+                    result_ref[3 * row + d, mine, :] = result_ref[3 * row + d, mine, :] + piece
+            if order == 3:
+                half_copy(row).start()
             return carry
 
-        lax.fori_loop(0, 9, step, 0)
+        lax.fori_loop(0, 3, step, 0)
 
     shift_some(0, 6)
     gather.pass_x(0)
     gather.pass_z(1)
+    add_hop(0)
     shift_some(6, 11)
     gather.pass_z(3)
     shift_some(11, 16)
     gather.pass_z(2)
+    add_hop(1)
     gather.take(0)
-    multiply(0)
-    for k in (1, 3, 2):
+    multiply(0, 0)
+    for order, k in ((1, 1), (2, 3), (3, 2)):
         gather.pass_x(k)
         gather.take(k)
-        multiply(k)
+        if order < 3:
+            add_hop(order + 1)
+        multiply(k, order)
+    hops[4].wait_recv()
     gather.drain()
-
-
-def outer(grad, gathered):
+    for hop in hops:
+        hop.wait_send()
+    for row in range(3):
+        half_copy(row).wait()
+
+
+def outer(grad, gathered, parts):
     pixels, channels = grad.shape
+    rows = parts.shape[0] // 2
     dma = pltpu.SemaphoreType.DMA
     return pl.pallas_call(
         outer_kernel,
-        out_shape=jax.ShapeDtypeStruct((9, channels, channels), jnp.float32),
-        in_specs=[pl.BlockSpec(memory_space=VM)] * 2,
-        out_specs=pl.BlockSpec(memory_space=VM),
+        out_shape=(
+            jax.ShapeDtypeStruct((9, channels, channels), jnp.float32),
+            jax.ShapeDtypeStruct(parts.shape, jnp.float32),
+        ),
+        in_specs=[pl.BlockSpec(memory_space=VM)] * 3,
+        out_specs=(pl.BlockSpec(memory_space=VM),) * 2,
         scratch_shapes=[
             VM((16, pixels, channels), jnp.bfloat16),
-            VM((3, channels, 18 * pixels), jnp.bfloat16),
+            VM((3 * channels // 2, 18 * pixels), jnp.bfloat16),
+            VM((3, rows, 128), jnp.float32),
+            VM((4, rows, 128), jnp.float32),
             dma((15,)),
             dma((16,)),
+            dma((3,)),
+            dma((3,)),
+            dma((5,)),
+            dma((5,)),
         ],
         compiler_params=pltpu.CompilerParams(
             collective_id=2, has_side_effects=True, vmem_limit_bytes=48 * 2**20
         ),
-        cost_estimate=pl.CostEstimate(
-            flops=2 * 9 * 16 * pixels * channels * channels,
-            bytes_accessed=20 * 2**20,
-            transcendentals=0,
-        ),
         name="outer",
-    )(grad, gathered)
+    )(grad, gathered, parts)
 
 
 def body16(
@@ -599,11 +676,17 @@
     scaled = (grad_hsum / (1.0 + covered)).reshape(tile_faces, length, channels)
     slot_grads = (jnp.take(scaled, recv_slot, axis=0) * validity[..., None]).astype(jnp.bfloat16)
     first_part, second_part = encoder_backward(saved, slot_grads, encoder_first, encoder_second)
-    parts = (gain_part, first_part, second_part)
-    grad_pred, parts = lax.optimization_barrier((grad_pred, parts))
-    reduced = lax.psum(parts, "tile")
-    grad_kernel = outer(grad_pred, gathered)
-    return (grad_kernel, reduced[0], reduced[1], reduced[2])
+    parts = (second_part, first_part, gain_part)
+    flat = jnp.concatenate([part.reshape(-1, 128) for part in parts], axis=0)
+    flat = jnp.pad(flat, ((0, -flat.shape[0] % 16), (0, 0)))
+    grad_kernel, total = outer(grad_pred, gathered, flat)
+    sums = []
+    at = 0
+    for part in parts:
+        count = part.size // 128
+        sums.append(total[at : at + count].reshape(part.shape))
+        at += count
+    return (grad_kernel, sums[2], sums[1], sums[0])
 
 
 def body(

time: 194 us -> 143 us (0.74)
  blocking collectives: 34.2 us -> 0 us
  waiting for transfers between devices: 14.5 us -> 0 us
  between operations: 15.1 us -> 1.7 us
  local copies, waits for them, and re-layouts: 15.6 us -> 23 us
  matrix products: 11.8 us -> 17.5 us
  Pallas kernels: 94.4 us -> 90.1 us
    psum x1 -> x0, blocking collectives: 34.2 us -> none  [body16(): reduced = lax.psum(parts, 'tile')]
    psum x1 -> x0, waiting for transfers between devices: 14.5 us -> none  [body16(): reduced = lax.psum(parts, 'tile')]
    reshape x0 -> x5, local copies, waits for them, and re-layouts: none -> 5.6 us  [the longest x2 3.17 us: body16(): flat = jnp.concatenate([part.reshape(-1, 128) for part in parts], axis=0)]
    pallas_call x1, Pallas kernels: 52.3 us -> 47.9 us  [outer(): pl.pallas_call(outer_kernel, out_shape=(jax.ShapeDtypeStruct((9, channels...]
    gather x2, local copies, waits for them, and re-layouts: 0.97 us -> 4.7 us  [body16(): jnp.take(scaled, recv_slot, axis=0) * validity[..., None]]
    dot_general x3, matrix products: 0.92 us -> 4.15 us  [taps_weight_grad(): jnp.einsum('flgi,flgo->gio', shifted, cotangent, preferred_element_type=j...]
    dot_general x3, matrix products: 2.21 us -> 4.34 us  [taps_input_grad(): jnp.einsum('flgo,gio->flgi', cotangent, weight[shift_tap], preferred_elem...]
    unnamed x37 -> x35, local copies, waits for them, and re-layouts: 9 us -> 8.91 us
  transfers between devices with their start and end apart: 1 -> 0, of which waited for: 1 -> 0; matrix products, arithmetic and copies ran while one was open for 0% -> 0% of each run, Pallas kernels for 27% -> 0%
where the time goes in v2:
time: 143 us; the launch traced here: 142 us
  Pallas kernels  90.1 us (63%)
  local copies, waits for them, and re-layouts  23 us (16%)
  matrix products  17.5 us (12%)
  other arithmetic  10.2 us (7%)
  between operations  1.7 us (1%)
    pallas_call x1, Pallas kernels, outer(): pl.pallas_call(outer_kernel, out_shape=(jax.ShapeDtypeStruct((9, channels...  47.9 us
    pallas_call x1, Pallas kernels, middle(): pl.pallas_call(middle_kernel, out_shape=(jax.ShapeDtypeStruct((pixels, ch...  31.4 us
    pallas_call x1, Pallas kernels, exchange(): pl.pallas_call(lambda *refs: exchange_kernel(count, *refs), out_shape=jax...  10.8 us
    unnamed x35, local copies, waits for them, and re-layouts  8.91 us
    dot_general x6, matrix products, taps_forward(): jnp.einsum('flgi,gio->flgo', shifted, weight[shift_tap], preferred_elemen...  6.4 us
    gather x2, local copies, waits for them, and re-layouts, body16(): jnp.take(scaled, recv_slot, axis=0) * validity[..., None]  4.7 us
    dot_general x3, matrix products, taps_input_grad(): jnp.einsum('flgo,gio->flgi', cotangent, weight[shift_tap], preferred_elem...  4.34 us
    dot_general x3, matrix products, taps_weight_grad(): jnp.einsum('flgi,flgo->gio', shifted, cotangent, preferred_element_type=j...  4.15 us

profile of v2, /device:TPU:0, one launch (start us, length us, event | category | flops | bytes accessed | tf_op | source)
XLA Modules:
  0.0 142.5 jit_solution(16418404563865447545)
XLA Ops:
  1.3 0.7 convert_bitcast_fusion
  2.0 0.7 fusion.50
  2.7 0.8 select_reduce_fusion.2
  3.6 0.7 multiply_add_fusion
  4.2 0.8 select_reduce_fusion.1
  5.1 0.3 convolution_convert_fusion
  5.4 0.7 copy.41
  6.1 10.8 %exchange.1 = bf16[16,32,128]{2,1,0:T(8,128)(2,1)} custom-call(bf16[16,32,128]{2,1,0:T(8,128)(2,1)} %bitcast.160), custom_call_target="tpu_custom_call" | custom-call | tf_op jit(solution)/shard_map/exchange/pallas_call | solution.py:191
  16.9 0.9 slice.88
  17.8 0.8 slice.89
  19.3 0.2 copy.67
  19.5 1.2 fusion.39
  20.7 1.1 convolution_add_fusion.1
  21.8 2.2 %multiply_convert_fusion = (bf16[32,8,8,48]{3,0,1,2:T(8,128)(2,1)S(1)}, f32[32,8,8,48]{3,0,1,2:T(8,128)}) fusion(f32[8,32,8,48]{3,1,2,0:T(8,128)S(1)} %convolution_add_fusion.1, bf16[3,8,16,48]{3,2,1,0:T(8,128)(2,1)} %param.20, bf16[32,8,8,16]{0,3,2,1:T(8,128)(2,1)S(1)} %bitcast.156), kind=kOutput, calls=%fused_computation.29 | convolution fusion | flops 3342336 | bytes 1900544 | tf_op jit(solution)/shard_map/flgi,gio->flgo/dot_general | solution.py:42
  24.0 1.3 fusion.28
  25.4 0.3 convolution_add_fusion.3
  25.7 0.3 fusion.8
  26.0 0.3 copy.47
  26.3 0.4 convert_element_type.100
  27.0 0.3 multiply_reduce_fusion.2
  27.6 1.7 %copy-done.1 = bf16[9,384,384]{2,1,0:T(8,128)(2,1)S(1)} copy-done((bf16[9,384,384]{2,1,0:T(8,128)(2,1)S(1)}, bf16[9,384,384]{2,1,0:T(8,128)(2,1)}, u32[]{:S(2)}) %copy-start.1) | copy-done | bytes 2654232
  29.3 0.9 copy-done.4
  30.3 31.4 %middle.1 = (f32[256,384]{1,0:T(8,128)S(1)}, bf16[256,384]{1,0:T(8,128)(2,1)S(1)}, bf16[16,384,256]{2,1,0:T(8,128)(2,1)S(1)}) custom-call(bf16[256,384]{1,0:T(8,128)(2,1)S(1)} %multiply_convert_fusion.1.act_ref, bf16[256,384]{1,0:T(8,128)(2,1)S(1)} %bitcast.152, bf16[256,384]{1,0:T(8,128)(2,1)S(1)} %bitcast.153, f32[256,1]{1,0:T(8,128)S(1)} %copy.52.weight_ref, ...), custom_call_target="tpu_custom_call" | custom-call | tf_op jit(solution)/shard_map/middle/pallas_call | solution.py:406
  61.7 0.7 copy-done.5
  62.4 0.4 multiply_reduce_fusion.1
  62.8 1.0 divide_bitcast_fusion
  63.8 2.3 %gather_fusion = f32[32,8,384]{2,1,0:T(8,128)} fusion(f32[32,8,384]{2,1,0:T(8,128)} %divide_bitcast_fusion, s32[1024]{0:T(1024)S(1)} %pad_clamp_fusion), kind=kCustom, calls=%fused_computation | custom fusion | bytes 786560 | tf_op jit(solution)/shard_map/jit(_take)/gather | solution.py:677
  66.2 2.4 %gather.7 = f32[32,8,8,48]{3,2,1,0:T(8,128)} reshape(f32[32,8,384]{2,1,0:T(8,128)} %gather_fusion) | data formatting | bytes 786432 | tf_op jit(solution)/shard_map/jit(_take)/gather | solution.py:677
  68.5 1.9 %fusion.11 = bf16[32,8,8,48]{3,0,1,2:T(8,128)(2,1)S(1)} fusion(f32[32,8,8,48]{3,2,1,0:T(8,128)} %gather.7, f32[32,8]{0,1:T(8,128)S(1)} %get-tuple-element.23, pred[32]{0:T(512)(128)(4,1)S(1)} %and_bitcast_fusion), kind=kLoop, calls=%fused_computation.28 | loop fusion | flops 294912 | bytes 590880 | tf_op jit(solution)/shard_map/convert_element_type | solution.py:677
  70.4 1.5 %convolution_bitcast_fusion.3 = f32[1,8,48,48]{3,2,1,0:T(8,128)S(1)} fusion(bf16[32,8,8,48]{3,0,1,2:T(8,128)(2,1)S(1)} %fusion.11, bf16[32,8,8,48]{3,0,1,2:T(8,128)(2,1)} %copy-done.9), kind=kOutput, calls=%fused_computation.17 | convolution fusion | flops 7077888 | bytes 663552 | tf_op jit(solution)/shard_map/flgi,flgo->gio/dot_general | solution.py:60
  71.9 1.4 convolution_bitcast_fusion.5
  73.3 1.3 convolution_bitcast_fusion.4
  74.6 0.9 pad_maximum_fusion
  75.5 2.1 %reshape.191 = f32[432,128]{1,0:T(8,128)} reshape(f32[3,8,48,48]{3,2,1,0:T(8,128)} %pad_maximum_fusion) | data formatting | bytes 442368 | tf_op jit(solution)/shard_map/reshape | solution.py:680
  77.6 1.4 %convolution_bitcast_fusion.2 = f32[32,8,8,48]{3,0,1,2:T(8,128)S(1)} fusion(bf16[32,8,8,48]{3,0,1,2:T(8,128)(2,1)} %copy-done.7, bf16[3,8,48,48]{3,2,1,0:T(8,128)(2,1)S(1)} %copy-done.13), kind=kOutput, calls=%fused_computation.3 | convolution fusion | flops 9437184 | bytes 688128 | tf_op jit(solution)/shard_map/flgo,gio->flgi/dot_general | solution.py:68
  79.1 1.4 convolution_bitcast_fusion
  80.5 1.5 %fusion.7 = f32[32,8,8,48]{3,0,1,2:T(8,128)S(1)} fusion(bf16[32,8,8,48]{3,0,1,2:T(8,128)(2,1)S(1)} %copy-done.8, f32[32,8,8,48]{3,0,1,2:T(8,128)S(1)} %copy-done.15, f32[32,6,8,48]{3,0,1,2:T(8,128)S(1)} %slice.95, f32[32,6,8,48]{3,0,1,2:T(8,128)S(1)} %slice.94, bf16[3,8,48,48]{3,2,1,0:T(8,128)(2,1)} %param.21), kind=kOutput, calls=%fused_computation.15 | convolution fusion | flops 10616832 | bytes 4161536 | tf_op jit(solution)/shard_map/flgo,gio->flgi/dot_general | solution.py:68
  82.1 0.7 convolution_bitcast_fusion.6
  82.8 0.7 convolution_bitcast_fusion.8
  83.5 0.7 convolution_bitcast_fusion.7
  84.2 0.7 pad_maximum_fusion.1
  84.9 1.1 reshape.192
  86.0 1.0 select_maximum_fusion.parts_ref
  86.9 47.9 %outer.1 = (f32[9,384,384]{2,1,0:T(8,128)}, f32[592,128]{1,0:T(8,128)S(1)}) custom-call(bf16[256,384]{1,0:T(8,128)(2,1)S(1)} %copy-done.6, bf16[16,384,256]{2,1,0:T(8,128)(2,1)S(1)} %get-tuple-element.10.gathered_ref, f32[592,128]{1,0:T(8,128)S(1)} %select_maximum_fusion.parts_ref), custom_call_target="tpu_custom_call" | custom-call | tf_op jit(solution)/shard_map/outer/pallas_call | solution.py:568
  134.8 0.6 slice_bitcast_fusion
  135.4 0.8 reshape.195
  136.2 1.1 reshape.196
  137.2 5.2 %copy.97 = f32[9,384,384]{2,1,0:T(8,128)} copy(f32[9,384,384]{2,1,0:T(8,128)} %get-tuple-element.33) | data formatting | bytes 10616832
  (54 shorter events, 1.5 us)
Async XLA Ops:
  0.6 4.5 %copy-start = (bf16[16,8,128]{2,1,0:T(8,128)(2,1)S(1)}, bf16[16,8,128]{2,1,0:T(8,128)(2,1)}, u32[]{:S(2)}) copy-start(bf16[16,8,128]{2,1,0:T(8,128)(2,1)} %param.12) | copy-start | bytes 98308
  19.5 5.9 %copy-start.10 = (bf16[32,8,128]{0,2,1:T(8,128)(2,1)}, bf16[32,8,128]{0,2,1:T(8,128)(2,1)S(1)}, u32[]{:S(2)}) copy-start(bf16[32,8,128]{0,2,1:T(8,128)(2,1)S(1)} %copy.67) | copy-start | bytes 196612
  19.5 5.9 %copy-start.12 = (bf16[3,8,48,48]{3,2,1,0:T(8,128)(2,1)S(1)}, bf16[3,8,48,48]{3,2,1,0:T(8,128)(2,1)}, u32[]{:S(2)}) copy-start(bf16[3,8,48,48]{3,2,1,0:T(8,128)(2,1)} %param.21) | copy-start | bytes 331780
  24.0 3.4 %copy-start.9 = (bf16[32,8,8,48]{3,0,1,2:T(8,128)(2,1)}, bf16[32,8,8,48]{3,0,1,2:T(8,128)(2,1)S(1)}, u32[]{:S(2)}) copy-start(bf16[32,8,8,48]{3,0,1,2:T(8,128)(2,1)S(1)} %get-tuple-element.25) | copy-start | bytes 589828
  24.0 3.0 %copy-start.2 = (bf16[1,256,384]{2,1,0:T(8,128)(2,1)S(1)}, bf16[1,256,384]{2,1,0:T(8,128)(2,1)}, u32[]{:S(2)}) copy-start(bf16[1,256,384]{2,1,0:T(8,128)(2,1)} %param.18) | copy-start | bytes 589828
  24.0 3.0 %copy-start.3 = (bf16[1,256,384]{2,1,0:T(8,128)(2,1)S(1)}, bf16[1,256,384]{2,1,0:T(8,128)(2,1)}, u32[]{:S(2)}) copy-start(bf16[1,256,384]{2,1,0:T(8,128)(2,1)} %param.19) | copy-start | bytes 589828
  24.0 3.4 %copy-start.14 = (f32[384]{0:T(512)S(1)}, f32[384]{0:T(512)}, u32[]{:S(2)}) copy-start(f32[384]{0:T(512)} %param.23) | copy-start | bytes 4612
  27.6 1.8 %copy-start.1 = (bf16[9,384,384]{2,1,0:T(8,128)(2,1)S(1)}, bf16[9,384,384]{2,1,0:T(8,128)(2,1)}, u32[]{:S(2)}) copy-start(bf16[9,384,384]{2,1,0:T(8,128)(2,1)} %kernel_ref.1) | copy-start | bytes 7962628
  29.3 0.9 copy-start.4
  61.7 0.7 copy-start.5
  62.8 14.8 %copy-start.13 = (bf16[3,8,48,48]{3,2,1,0:T(8,128)(2,1)S(1)}, bf16[3,8,48,48]{3,2,1,0:T(8,128)(2,1)}, u32[]{:S(2)}) copy-start(bf16[3,8,48,48]{3,2,1,0:T(8,128)(2,1)} %param.21) | copy-start | bytes 331780
  70.4 2.9 %copy-start.7 = (bf16[32,8,8,48]{3,0,1,2:T(8,128)(2,1)}, bf16[32,8,8,48]{3,0,1,2:T(8,128)(2,1)S(1)}, u32[]{:S(2)}) copy-start(bf16[32,8,8,48]{3,0,1,2:T(8,128)(2,1)S(1)} %fusion.11) | copy-start | bytes 589828
  77.6 2.9 %copy-start.8 = (bf16[32,8,8,48]{3,0,1,2:T(8,128)(2,1)S(1)}, bf16[32,8,8,48]{3,0,1,2:T(8,128)(2,1)}, u32[]{:S(2)}) copy-start(bf16[32,8,8,48]{3,0,1,2:T(8,128)(2,1)} %copy-done.7) | copy-start | bytes 589828
  77.6 3.0 %copy-start.15 = (f32[32,8,8,48]{3,0,1,2:T(8,128)S(1)}, f32[32,8,8,48]{3,0,1,2:T(8,128)}, u32[]{:S(2)}) copy-start(f32[32,8,8,48]{3,0,1,2:T(8,128)} %get-tuple-element.26) | copy-start | bytes 1179652
  79.1 3.0 %copy-start.11 = (bf16[32,8,128]{0,2,1:T(8,128)(2,1)S(1)}, bf16[32,8,128]{0,2,1:T(8,128)(2,1)}, u32[]{:S(2)}) copy-start(bf16[32,8,128]{0,2,1:T(8,128)(2,1)} %copy-done.10) | copy-start | bytes 196612
  80.5 6.4 %copy-start.6 = (bf16[256,384]{1,0:T(8,128)(2,1)S(1)}, bf16[256,384]{1,0:T(8,128)(2,1)}, u32[]{:S(2)}) copy-start(bf16[256,384]{1,0:T(8,128)(2,1)} %copy-done.5) | copy-start | bytes 589828

commit v3 on v2

--- a/solution.py
+++ b/solution.py
@@ -209,9 +209,15 @@
         self.me = lax.axis_index("tile")
         self.core = lax.rem(self.me, 2)
         self.x = lax.rem(self.me // 2, 2)
-        self.z = self.me // 4
-        self.x_peer = self.z * 4 + (1 - self.x) * 2 + self.core
-        self.sibling = self.z * 4 + self.x * 2 + (1 - self.core)
+        self.z = z = self.me // 4
+        self.x_peer = z * 4 + (1 - self.x) * 2 + self.core
+        self.sibling = z * 4 + self.x * 2 + (1 - self.core)
+        self.planes = [
+            z,
+            jnp.where(z == 0, 1, z - 1),
+            jnp.where(z == 0, 2, jnp.where(z == 3, 1, z + 1)),
+            jnp.where(z < 2, 3, 0),
+        ]
 
     def copy(self, chunk, to, index):
         return pltpu.make_async_remote_copy(
@@ -223,34 +229,68 @@
             device_id_type=MESH,
         )
 
-    def at(self, back, x, core):
-        return lax.rem(self.z + 4 - back, 4) * 4 + x * 2 + core
+    def at(self, step, x, core):
+        return self.planes[step] * 4 + x * 2 + core
+
+    def along(self, step):
+        place = lax.rem(self.me, 4)
+        onward = jnp.where(self.planes[step] < self.z, self.z + 1, self.z - 1)
+        valid = (onward >= 0) & (onward <= 3)
+        return jnp.clip(onward, 0, 3) * 4 + place, valid
 
     def start(self):
-        self.copy(self.me, self.x_peer, 3).start()
-        self.copy(self.me, self.sibling, 4).start()
-        for k in (1, 3, 2):
-            to = lax.rem(self.z + k, 4) * 4 + self.x * 2 + self.core
-            self.copy(self.me, to, k - 1).start()
-
-    def pass_z(self, back):
-        chunk = self.at(back, self.x, self.core)
+        place = lax.rem(self.me, 4)
+
+        @pl.when(self.z < 3)
+        def _():
+            self.copy(self.me, jnp.minimum(self.z + 1, 3) * 4 + place, 0).start()
+
+        @pl.when(self.z > 0)
+        def _():
+            self.copy(self.me, jnp.maximum(self.z - 1, 0) * 4 + place, 1).start()
+
+        self.copy(self.me, self.x_peer, 2).start()
+        self.copy(self.me, self.sibling, 3).start()
+
+    def pass_z(self, step):
+        chunk = self.at(step, self.x, self.core)
         self.copy(chunk, self.x_peer, 0).wait_recv()
-        self.copy(chunk, self.x_peer, 5 + 2 * (back - 1)).start()
-        self.copy(chunk, self.sibling, 6 + 2 * (back - 1)).start()
-
-    def pass_x(self, back):
-        chunk = self.at(back, 1 - self.x, self.core)
+        to, valid = self.along(step)
+
+        @pl.when(valid)
+        def _():
+            self.copy(chunk, to, 3 + step).start()
+
+        self.copy(chunk, self.x_peer, 6 + step).start()
+        self.copy(chunk, self.sibling, 9 + step).start()
+
+    def pass_x(self, step):
+        chunk = self.at(step, 1 - self.x, self.core)
         self.copy(chunk, self.sibling, 0).wait_recv()
-        self.copy(chunk, self.sibling, 11 + back).start()
-
-    def take(self, back):
+        self.copy(chunk, self.sibling, 13 + step).start()
+
+    def take(self, step):
         for x in (self.x, 1 - self.x):
-            chunk = self.at(back, x, 1 - self.core)
+            chunk = self.at(step, x, 1 - self.core)
             self.copy(chunk, self.sibling, 0).wait_recv()
 
     def drain(self):
-        for index in range(15):
+        @pl.when(self.z < 3)
+        def _():
+            self.copy(self.me, self.sibling, 0).wait_send()
+
+        @pl.when(self.z > 0)
+        def _():
+            self.copy(self.me, self.sibling, 1).wait_send()
+
+        for step in range(1, 4):
+            _, valid = self.along(step)
+
+            @pl.when(valid)
+            def _():
+                self.copy(self.me, self.sibling, 3 + step).wait_send()
+
+        for index in (2, 3, 7, 8, 9, 10, 11, 12, 13, 14, 15, 16):
             self.copy(self.me, self.sibling, index).wait_send()
 
 
@@ -368,9 +408,10 @@
             values, kernel_ref[tap], (((1,), (1,)), ((), ())), preferred_element_type=f32
         )
 
+    gather.pass_z(1)
     sums = [back(grad, 3 + d) for d in range(3)]
-    for k in (1, 3, 2):
-        gather.pass_z(k)
+    gather.pass_x(0)
+    gather.pass_z(2)
 
     @pl.when(me > 0)
     def _():
@@ -383,10 +424,12 @@
     above, below = halo_g[0], halo_g[1]
     sums = [sums[d] + back(below, d) + back(above, 6 + d) for d in range(3)]
     flows_ref[...] = sums[1] + moved(sums[0], 1, 0) + moved(sums[2], -1, 0)
-    for k in (0, 1, 3, 2):
-        gather.pass_x(k)
-    for k in (0, 1, 3, 2):
-        gather.take(k)
+    gather.pass_x(1)
+    gather.pass_z(3)
+    gather.pass_x(2)
+    gather.pass_x(3)
+    for step in range(4):
+        gather.take(step)
     gather.drain()
 
     @pl.when(me > 0)
@@ -415,7 +458,7 @@
         scratch_shapes=[
             VM((2, pixels, channels), jnp.bfloat16),
             VM((2, pixels, channels), jnp.bfloat16),
-            dma((15,)),
+            dma((17,)),
             dma((16,)),
             dma((2,)),
             dma((2,)),
@@ -423,7 +466,7 @@
             dma((2,)),
         ],
         compiler_params=pltpu.CompilerParams(
-            collective_id=1, has_side_effects=True, vmem_limit_bytes=40 * 2**20
+            collective_id=1, has_side_effects=True, vmem_limit_bytes=14 * 2**20
         ),
         name="middle",
     )(activated, clean, noise, pixel_weight, kernel)
@@ -516,8 +559,8 @@
             device_id_type=MESH,
         )
 
-    def multiply(back, order):
-        base = lax.rem(z + 4 - back, 4) * 4
+    def multiply(order):
+        base = gather.planes[order] * 4
         right = grads[pl.ds(base, 4)].reshape(4 * pixels, channels)
 
         def step(row, carry):
@@ -536,23 +579,28 @@
 
         lax.fori_loop(0, 3, step, 0)
 
-    shift_some(0, 6)
+    shift_some(0, 4)
+    gather.pass_z(1)
     gather.pass_x(0)
-    gather.pass_z(1)
     add_hop(0)
-    shift_some(6, 11)
-    gather.pass_z(3)
-    shift_some(11, 16)
+    shift_some(4, 10)
     gather.pass_z(2)
+    gather.pass_x(1)
+    shift_some(10, 16)
     add_hop(1)
     gather.take(0)
-    multiply(0, 0)
-    for order, k in ((1, 1), (2, 3), (3, 2)):
-        gather.pass_x(k)
-        gather.take(k)
-        if order < 3:
-            add_hop(order + 1)
-        multiply(k, order)
+    gather.pass_z(3)
+    multiply(0)
+    gather.pass_x(2)
+    add_hop(2)
+    gather.take(1)
+    multiply(1)
+    gather.pass_x(3)
+    add_hop(3)
+    gather.take(2)
+    multiply(2)
+    gather.take(3)
+    multiply(3)
     hops[4].wait_recv()
     gather.drain()
     for hop in hops:
@@ -578,7 +626,7 @@
             VM((3 * channels // 2, 18 * pixels), jnp.bfloat16),
             VM((3, rows, 128), jnp.float32),
             VM((4, rows, 128), jnp.float32),
-            dma((15,)),
+            dma((17,)),
             dma((16,)),
             dma((3,)),
             dma((3,)),
@@ -586,7 +634,7 @@
             dma((5,)),
         ],
         compiler_params=pltpu.CompilerParams(
-            collective_id=2, has_side_effects=True, vmem_limit_bytes=48 * 2**20
+            collective_id=2, has_side_effects=True, vmem_limit_bytes=24 * 2**20
         ),
         name="outer",
     )(grad, gathered, parts)

time: 143 us -> 145 us (1.014)
  local copies, waits for them, and re-layouts: 23 us -> 25.3 us
    pallas_call x1, Pallas kernels: 47.9 us -> 42.1 us  [outer(): pl.pallas_call(outer_kernel, out_shape=(jax.ShapeDtypeStruct((9, channels...]
    pallas_call x1, Pallas kernels: 31.4 us -> 35.9 us  [middle(): pl.pallas_call(middle_kernel, out_shape=(jax.ShapeDtypeStruct((pixels, ch...]
    unnamed x35 -> x37, local copies, waits for them, and re-layouts: 8.91 us -> 11.2 us
where the time goes in v3:
time: 145 us; the launch traced here: 143 us
  Pallas kernels  88.7 us (61%)
  local copies, waits for them, and re-layouts  25.3 us (17%)
  matrix products  17.5 us (12%)
  other arithmetic  10.2 us (7%)
  between operations  1.71 us (1%)
    pallas_call x1, Pallas kernels, outer(): pl.pallas_call(outer_kernel, out_shape=(jax.ShapeDtypeStruct((9, channels...  42.1 us
    pallas_call x1, Pallas kernels, middle(): pl.pallas_call(middle_kernel, out_shape=(jax.ShapeDtypeStruct((pixels, ch...  35.9 us
    unnamed x37, local copies, waits for them, and re-layouts  11.2 us
    pallas_call x1, Pallas kernels, exchange(): pl.pallas_call(lambda *refs: exchange_kernel(count, *refs), out_shape=jax...  10.8 us
    dot_general x6, matrix products, taps_forward(): jnp.einsum('flgi,gio->flgo', shifted, weight[shift_tap], preferred_elemen...  6.4 us
    gather x2, local copies, waits for them, and re-layouts, body16(): jnp.take(scaled, recv_slot, axis=0) * validity[..., None]  4.7 us
    dot_general x3, matrix products, taps_input_grad(): jnp.einsum('flgo,gio->flgi', cotangent, weight[shift_tap], preferred_elem...  4.34 us
    dot_general x3, matrix products, taps_weight_grad(): jnp.einsum('flgi,flgo->gio', shifted, cotangent, preferred_element_type=j...  4.15 us

profile of v3, /device:TPU:0, one launch (start us, length us, event | category | flops | bytes accessed | tf_op | source)
XLA Modules:
  0.0 143.5 jit_solution(5098323614489621992)
XLA Ops:
  1.3 0.7 convert_bitcast_fusion
  2.0 0.7 fusion.50
  2.7 0.8 select_reduce_fusion.2
  3.6 0.7 multiply_add_fusion
  4.2 0.8 select_reduce_fusion.1
  5.1 0.3 convolution_convert_fusion
  5.4 0.7 copy.41
  6.1 10.8 %exchange.1 = bf16[16,32,128]{2,1,0:T(8,128)(2,1)} custom-call(bf16[16,32,128]{2,1,0:T(8,128)(2,1)} %bitcast.160), custom_call_target="tpu_custom_call" | custom-call | tf_op jit(solution)/shard_map/exchange/pallas_call | solution.py:191
  16.9 0.9 slice.88
  17.8 0.8 slice.89
  19.5 1.2 fusion.39
  20.7 1.1 convolution_add_fusion.1
  21.8 2.2 %multiply_convert_fusion = (bf16[32,8,8,48]{3,0,1,2:T(8,128)(2,1)S(1)}, f32[32,8,8,48]{3,0,1,2:T(8,128)}) fusion(f32[8,32,8,48]{3,1,2,0:T(8,128)S(1)} %convolution_add_fusion.1, bf16[3,8,16,48]{3,2,1,0:T(8,128)(2,1)} %param.20, bf16[32,8,8,16]{0,3,2,1:T(8,128)(2,1)S(1)} %bitcast.156), kind=kOutput, calls=%fused_computation.29 | convolution fusion | flops 3342336 | bytes 1900544 | tf_op jit(solution)/shard_map/flgi,gio->flgo/dot_general | solution.py:42
  24.0 1.3 fusion.28
  25.4 0.3 convolution_add_fusion.3
  25.7 0.3 fusion.8
  26.0 0.3 copy.47
  26.3 0.4 convert_element_type.100
  27.0 0.4 multiply_reduce_fusion.2
  27.6 1.7 %copy-done.2 = bf16[9,384,384]{2,1,0:T(8,128)(2,1)S(1)} copy-done((bf16[9,384,384]{2,1,0:T(8,128)(2,1)S(1)}, bf16[9,384,384]{2,1,0:T(8,128)(2,1)}, u32[]{:S(2)}) %copy-start.2) | copy-done | bytes 2654232
  29.3 0.9 copy-done.5
  30.3 35.9 %middle.1 = (f32[256,384]{1,0:T(8,128)S(1)}, bf16[256,384]{1,0:T(8,128)(2,1)S(1)}, bf16[16,384,256]{2,1,0:T(8,128)(2,1)S(1)}) custom-call(bf16[256,384]{1,0:T(8,128)(2,1)S(1)} %multiply_convert_fusion.1.act_ref, bf16[256,384]{1,0:T(8,128)(2,1)S(1)} %bitcast.152, bf16[256,384]{1,0:T(8,128)(2,1)S(1)} %bitcast.153, f32[256,1]{1,0:T(8,128)S(1)} %copy.52.weight_ref, ...), custom_call_target="tpu_custom_call" | custom-call | tf_op jit(solution)/shard_map/middle/pallas_call | solution.py:449
  66.2 0.7 copy-done.6
  66.9 0.4 multiply_reduce_fusion.1
  67.3 1.0 divide_bitcast_fusion
  68.3 2.3 %gather_fusion = f32[32,8,384]{2,1,0:T(8,128)} fusion(f32[32,8,384]{2,1,0:T(8,128)} %divide_bitcast_fusion, s32[1024]{0:T(1024)S(1)} %pad_clamp_fusion), kind=kCustom, calls=%fused_computation | custom fusion | bytes 786560 | tf_op jit(solution)/shard_map/jit(_take)/gather | solution.py:725
  70.6 2.4 %gather.7 = f32[32,8,8,48]{3,2,1,0:T(8,128)} reshape(f32[32,8,384]{2,1,0:T(8,128)} %gather_fusion) | data formatting | bytes 786432 | tf_op jit(solution)/shard_map/jit(_take)/gather | solution.py:725
  73.0 1.9 %fusion.11 = bf16[32,8,8,48]{3,0,1,2:T(8,128)(2,1)S(1)} fusion(f32[32,8,8,48]{3,2,1,0:T(8,128)} %gather.7, f32[32,8]{0,1:T(8,128)S(1)} %get-tuple-element.23, pred[32]{0:T(512)(128)(4,1)S(1)} %and_bitcast_fusion), kind=kLoop, calls=%fused_computation.28 | loop fusion | flops 294912 | bytes 590880 | tf_op jit(solution)/shard_map/convert_element_type | solution.py:725
  74.9 1.5 %convolution_bitcast_fusion.3 = f32[1,8,48,48]{3,2,1,0:T(8,128)S(1)} fusion(bf16[32,8,8,48]{3,0,1,2:T(8,128)(2,1)S(1)} %fusion.11, bf16[32,8,8,48]{3,0,1,2:T(8,128)(2,1)} %copy-done.10), kind=kOutput, calls=%fused_computation.17 | convolution fusion | flops 7077888 | bytes 663552 | tf_op jit(solution)/shard_map/flgi,flgo->gio/dot_general | solution.py:60
  76.4 1.4 convolution_bitcast_fusion.5
  77.8 1.3 convolution_bitcast_fusion.4
  79.1 0.9 pad_maximum_fusion
  80.0 2.1 %reshape.191 = f32[432,128]{1,0:T(8,128)} reshape(f32[3,8,48,48]{3,2,1,0:T(8,128)} %pad_maximum_fusion) | data formatting | bytes 442368 | tf_op jit(solution)/shard_map/reshape | solution.py:728
  82.1 1.4 %convolution_bitcast_fusion.2 = f32[32,8,8,48]{3,0,1,2:T(8,128)S(1)} fusion(bf16[32,8,8,48]{3,0,1,2:T(8,128)(2,1)} %copy-done.8, bf16[3,8,48,48]{3,2,1,0:T(8,128)(2,1)S(1)} %copy-done.14), kind=kOutput, calls=%fused_computation.3 | convolution fusion | flops 9437184 | bytes 688128 | tf_op jit(solution)/shard_map/flgo,gio->flgi/dot_general | solution.py:68
  83.6 1.4 convolution_bitcast_fusion
  85.0 1.5 %fusion.7 = f32[32,8,8,48]{3,0,1,2:T(8,128)S(1)} fusion(bf16[32,8,8,48]{3,0,1,2:T(8,128)(2,1)S(1)} %copy-done.9, f32[32,8,8,48]{3,0,1,2:T(8,128)S(1)} %copy-done.16, f32[32,6,8,48]{3,0,1,2:T(8,128)S(1)} %slice.95, f32[32,6,8,48]{3,0,1,2:T(8,128)S(1)} %slice.94, bf16[3,8,48,48]{3,2,1,0:T(8,128)(2,1)} %param.21), kind=kOutput, calls=%fused_computation.15 | convolution fusion | flops 10616832 | bytes 4161536 | tf_op jit(solution)/shard_map/flgo,gio->flgi/dot_general | solution.py:68
  86.6 0.7 convolution_bitcast_fusion.6
  87.3 0.7 convolution_bitcast_fusion.8
  88.0 0.7 convolution_bitcast_fusion.7
  88.7 0.7 pad_maximum_fusion.1
  89.4 1.1 reshape.192
  90.4 1.0 select_maximum_fusion.parts_ref
  91.4 42.1 %outer.1 = (f32[9,384,384]{2,1,0:T(8,128)S(1)}, f32[592,128]{1,0:T(8,128)S(1)}) custom-call(bf16[256,384]{1,0:T(8,128)(2,1)S(1)} %copy-done.7, bf16[16,384,256]{2,1,0:T(8,128)(2,1)S(1)} %get-tuple-element.10.gathered_ref, f32[592,128]{1,0:T(8,128)S(1)} %select_maximum_fusion.parts_ref), custom_call_target="tpu_custom_call" | custom-call | tf_op jit(solution)/shard_map/outer/pallas_call | solution.py:616
  133.5 2.3 %copy-done.1 = f32[9,384,384]{2,1,0:T(8,128)} copy-done((f32[9,384,384]{2,1,0:T(8,128)}, f32[9,384,384]{2,1,0:T(8,128)S(1)}, u32[]{:S(2)}) %copy-start.1) | copy-done | bytes 5308440
  135.8 0.6 slice_bitcast_fusion
  136.4 0.8 reshape.195
  137.2 1.1 reshape.196
  138.2 5.2 %copy.97 = f32[9,384,384]{2,1,0:T(8,128)} copy(f32[9,384,384]{2,1,0:T(8,128)} %copy-done.1) | data formatting | bytes 10616832
  (56 shorter events, 1.7 us)
Async XLA Ops:
  0.6 4.5 %copy-start = (bf16[16,8,128]{2,1,0:T(8,128)(2,1)S(1)}, bf16[16,8,128]{2,1,0:T(8,128)(2,1)}, u32[]{:S(2)}) copy-start(bf16[16,8,128]{2,1,0:T(8,128)(2,1)} %param.12) | copy-start | bytes 98308
  19.5 5.9 %copy-start.11 = (bf16[32,8,128]{0,2,1:T(8,128)(2,1)}, bf16[32,8,128]{0,2,1:T(8,128)(2,1)S(1)}, u32[]{:S(2)}) copy-start(bf16[32,8,128]{0,2,1:T(8,128)(2,1)S(1)} %copy.67) | copy-start | bytes 196612
  19.5 5.9 %copy-start.13 = (bf16[3,8,48,48]{3,2,1,0:T(8,128)(2,1)S(1)}, bf16[3,8,48,48]{3,2,1,0:T(8,128)(2,1)}, u32[]{:S(2)}) copy-start(bf16[3,8,48,48]{3,2,1,0:T(8,128)(2,1)} %param.21) | copy-start | bytes 331780
  24.0 3.4 %copy-start.10 = (bf16[32,8,8,48]{3,0,1,2:T(8,128)(2,1)}, bf16[32,8,8,48]{3,0,1,2:T(8,128)(2,1)S(1)}, u32[]{:S(2)}) copy-start(bf16[32,8,8,48]{3,0,1,2:T(8,128)(2,1)S(1)} %get-tuple-element.25) | copy-start | bytes 589828
  24.0 3.0 %copy-start.3 = (bf16[1,256,384]{2,1,0:T(8,128)(2,1)S(1)}, bf16[1,256,384]{2,1,0:T(8,128)(2,1)}, u32[]{:S(2)}) copy-start(bf16[1,256,384]{2,1,0:T(8,128)(2,1)} %param.18) | copy-start | bytes 589828
  24.0 3.0 %copy-start.4 = (bf16[1,256,384]{2,1,0:T(8,128)(2,1)S(1)}, bf16[1,256,384]{2,1,0:T(8,128)(2,1)}, u32[]{:S(2)}) copy-start(bf16[1,256,384]{2,1,0:T(8,128)(2,1)} %param.19) | copy-start | bytes 589828
  24.0 3.4 %copy-start.15 = (f32[384]{0:T(512)S(1)}, f32[384]{0:T(512)}, u32[]{:S(2)}) copy-start(f32[384]{0:T(512)} %param.23) | copy-start | bytes 4612
  27.6 1.8 %copy-start.2 = (bf16[9,384,384]{2,1,0:T(8,128)(2,1)S(1)}, bf16[9,384,384]{2,1,0:T(8,128)(2,1)}, u32[]{:S(2)}) copy-start(bf16[9,384,384]{2,1,0:T(8,128)(2,1)} %kernel_ref.1) | copy-start | bytes 7962628
  29.3 0.9 copy-start.5
  66.2 0.7 copy-start.6
  67.3 14.8 %copy-start.14 = (bf16[3,8,48,48]{3,2,1,0:T(8,128)(2,1)S(1)}, bf16[3,8,48,48]{3,2,1,0:T(8,128)(2,1)}, u32[]{:S(2)}) copy-start(bf16[3,8,48,48]{3,2,1,0:T(8,128)(2,1)} %param.21) | copy-start | bytes 331780
  74.9 2.9 %copy-start.8 = (bf16[32,8,8,48]{3,0,1,2:T(8,128)(2,1)}, bf16[32,8,8,48]{3,0,1,2:T(8,128)(2,1)S(1)}, u32[]{:S(2)}) copy-start(bf16[32,8,8,48]{3,0,1,2:T(8,128)(2,1)S(1)} %fusion.11) | copy-start | bytes 589828
  82.1 2.9 %copy-start.9 = (bf16[32,8,8,48]{3,0,1,2:T(8,128)(2,1)S(1)}, bf16[32,8,8,48]{3,0,1,2:T(8,128)(2,1)}, u32[]{:S(2)}) copy-start(bf16[32,8,8,48]{3,0,1,2:T(8,128)(2,1)} %copy-done.8) | copy-start | bytes 589828
  82.1 3.0 %copy-start.16 = (f32[32,8,8,48]{3,0,1,2:T(8,128)S(1)}, f32[32,8,8,48]{3,0,1,2:T(8,128)}, u32[]{:S(2)}) copy-start(f32[32,8,8,48]{3,0,1,2:T(8,128)} %get-tuple-element.26) | copy-start | bytes 1179652
  83.6 3.0 %copy-start.12 = (bf16[32,8,128]{0,2,1:T(8,128)(2,1)S(1)}, bf16[32,8,128]{0,2,1:T(8,128)(2,1)}, u32[]{:S(2)}) copy-start(bf16[32,8,128]{0,2,1:T(8,128)(2,1)} %copy-done.11) | copy-start | bytes 196612
  85.0 6.4 %copy-start.7 = (bf16[256,384]{1,0:T(8,128)(2,1)S(1)}, bf16[256,384]{1,0:T(8,128)(2,1)}, u32[]{:S(2)}) copy-start(bf16[256,384]{1,0:T(8,128)(2,1)} %copy-done.6) | copy-start | bytes 589828
  133.5 2.3 %copy-start.1 = (f32[9,384,384]{2,1,0:T(8,128)}, f32[9,384,384]{2,1,0:T(8,128)S(1)}, u32[]{:S(2)}) copy-start(f32[9,384,384]{2,1,0:T(8,128)S(1)} %get-tuple-element.33) | copy-start | bytes 15925252

commit v4 on v3

--- a/solution.py
+++ b/solution.py
@@ -294,6 +294,57 @@
             self.copy(self.me, self.sibling, index).wait_send()
 
 
+class Spread:
+    def __init__(self, buf, send, recv):
+        self.buf, self.send_sem, self.recv_sem = buf, send, recv
+        self.me = lax.axis_index("tile")
+        self.core = lax.rem(self.me, 2)
+        self.x = lax.rem(self.me // 2, 2)
+        self.z = self.me // 4
+        self.x_peer = self.z * 4 + (1 - self.x) * 2 + self.core
+        self.sibling = self.z * 4 + self.x * 2 + (1 - self.core)
+
+    def copy(self, chunk, to, index):
+        return pltpu.make_async_remote_copy(
+            src_ref=self.buf.at[chunk],
+            dst_ref=self.buf.at[chunk],
+            send_sem=self.send_sem.at[index],
+            recv_sem=self.recv_sem.at[chunk],
+            device_id={"tile": to},
+            device_id_type=MESH,
+        )
+
+    def at(self, back, x, core):
+        return lax.rem(self.z + 4 - back, 4) * 4 + x * 2 + core
+
+    def start(self):
+        self.copy(self.me, self.x_peer, 3).start()
+        self.copy(self.me, self.sibling, 4).start()
+        for k in (1, 3, 2):
+            to = lax.rem(self.z + k, 4) * 4 + self.x * 2 + self.core
+            self.copy(self.me, to, k - 1).start()
+
+    def pass_z(self, back):
+        chunk = self.at(back, self.x, self.core)
+        self.copy(chunk, self.x_peer, 0).wait_recv()
+        self.copy(chunk, self.x_peer, 5 + 2 * (back - 1)).start()
+        self.copy(chunk, self.sibling, 6 + 2 * (back - 1)).start()
+
+    def pass_x(self, back):
+        chunk = self.at(back, 1 - self.x, self.core)
+        self.copy(chunk, self.sibling, 0).wait_recv()
+        self.copy(chunk, self.sibling, 11 + back).start()
+
+    def take(self, back):
+        for x in (self.x, 1 - self.x):
+            chunk = self.at(back, x, 1 - self.core)
+            self.copy(chunk, self.sibling, 0).wait_recv()
+
+    def drain(self):
+        for index in range(15):
+            self.copy(self.me, self.sibling, index).wait_send()
+
+
 def moved(values, offset, axis):
     extent = values.shape[axis]
     rolled = pltpu.roll(values, (-offset) % extent, axis)
@@ -356,7 +407,7 @@
         a_down.start()
 
     gathered_ref[me] = act_ref[...].T
-    gather = Gather(gathered_ref, gather_send, gather_recv)
+    gather = Spread(gathered_ref, gather_send, gather_recv)
     gather.start()
 
     @pl.when(me == 0)
@@ -408,10 +459,9 @@
             values, kernel_ref[tap], (((1,), (1,)), ((), ())), preferred_element_type=f32
         )
 
-    gather.pass_z(1)
     sums = [back(grad, 3 + d) for d in range(3)]
-    gather.pass_x(0)
-    gather.pass_z(2)
+    for k in (1, 3, 2):
+        gather.pass_z(k)
 
     @pl.when(me > 0)
     def _():
@@ -424,12 +474,10 @@
     above, below = halo_g[0], halo_g[1]
     sums = [sums[d] + back(below, d) + back(above, 6 + d) for d in range(3)]
     flows_ref[...] = sums[1] + moved(sums[0], 1, 0) + moved(sums[2], -1, 0)
-    gather.pass_x(1)
-    gather.pass_z(3)
-    gather.pass_x(2)
-    gather.pass_x(3)
-    for step in range(4):
-        gather.take(step)
+    for k in (0, 1, 3, 2):
+        gather.pass_x(k)
+    for k in (0, 1, 3, 2):
+        gather.take(k)
     gather.drain()
 
     @pl.when(me > 0)
@@ -458,7 +506,7 @@
         scratch_shapes=[
             VM((2, pixels, channels), jnp.bfloat16),
             VM((2, pixels, channels), jnp.bfloat16),
-            dma((17,)),
+            dma((15,)),
             dma((16,)),
             dma((2,)),
             dma((2,)),
@@ -640,6 +688,25 @@
     )(grad, gathered, parts)
 
 
+def settle_kernel(x_ref, o_ref, sems):
+    count = x_ref.shape[0]
+    for i in range(count):
+        pltpu.make_async_copy(x_ref.at[i], o_ref.at[i], sems.at[i]).start()
+    for i in range(count):
+        pltpu.make_async_copy(x_ref.at[i], o_ref.at[i], sems.at[i]).wait()
+
+
+def settle(values):
+    return pl.pallas_call(
+        settle_kernel,
+        out_shape=jax.ShapeDtypeStruct(values.shape, values.dtype),
+        in_specs=[pl.BlockSpec(memory_space=VM)],
+        out_specs=pl.BlockSpec(memory_space=pl.ANY),
+        scratch_shapes=[pltpu.SemaphoreType.DMA((values.shape[0],))],
+        name="settle",
+    )(values)
+
+
 def body16(
     sar_faces,
     dest_owner,
@@ -721,8 +788,14 @@
         conv_kernel,
     )
     gain_part, grad_hsum = norm_backward(flows, lifted, normed, inverse, norm_gain)
-    scaled = (grad_hsum / (1.0 + covered)).reshape(tile_faces, length, channels)
-    slot_grads = (jnp.take(scaled, recv_slot, axis=0) * validity[..., None]).astype(jnp.bfloat16)
+    scaled = (grad_hsum / (1.0 + covered)).astype(jnp.bfloat16)
+    target = recv_slot[:, None] * length + jnp.arange(length, dtype=jnp.int32)[None, :]
+    target = jnp.where(validity > 0, target, -1).reshape(-1)
+    picker = target[:, None] == jnp.arange(rows * columns, dtype=jnp.int32)[None, :]
+    slot_grads = jnp.dot(
+        picker.astype(jnp.bfloat16), scaled, preferred_element_type=jnp.float32
+    ).astype(jnp.bfloat16)
+    slot_grads = slot_grads.reshape(slot_total, length, channels)
     first_part, second_part = encoder_backward(saved, slot_grads, encoder_first, encoder_second)
     parts = (second_part, first_part, gain_part)
     flat = jnp.concatenate([part.reshape(-1, 128) for part in parts], axis=0)
@@ -734,7 +807,7 @@
         count = part.size // 128
         sums.append(total[at : at + count].reshape(part.shape))
         at += count
-    return (grad_kernel, sums[2], sums[1], sums[0])
+    return (settle(grad_kernel), sums[2], sums[1], sums[0])
 
 
 def body(

time: 145 us -> 137 us (0.945)
  local copies, waits for them, and re-layouts: 25.3 us -> 16.2 us
  other arithmetic: 10.2 us -> 6.52 us
  Pallas kernels: 88.7 us -> 92 us
  matrix products: 17.5 us -> 19.5 us
    unnamed x37 -> x32, local copies, waits for them, and re-layouts: 11.2 us -> 6.25 us
    pallas_call x0 -> x1, Pallas kernels: none -> 4.95 us  [settle(): pl.pallas_call(settle_kernel, out_shape=jax.ShapeDtypeStruct(values.shape...]
    gather x2 -> x0, local copies, waits for them, and re-layouts: 4.7 us -> none  [body16(): jnp.take(scaled, recv_slot, axis=0) * validity[..., None]]
    pallas_call x1, Pallas kernels: 35.9 us -> 31.4 us  [middle(): pl.pallas_call(middle_kernel, out_shape=(jax.ShapeDtypeStruct((pixels, ch...]
    pallas_call x1, Pallas kernels: 42.1 us -> 44.9 us  [outer(): pl.pallas_call(outer_kernel, out_shape=(jax.ShapeDtypeStruct((9, channels...]
    convert_element_type x2 -> x1, other arithmetic: 1.88 us -> 0.07 us  [body16(): masked = received * validity[..., None].astype(jnp.bfloat16)]
where the time goes in v4:
time: 137 us; the launch traced here: 136 us
  Pallas kernels  92 us (67%)
  matrix products  19.5 us (14%)
  local copies, waits for them, and re-layouts  16.2 us (12%)
  other arithmetic  6.52 us (5%)
  between operations  1.69 us (1%)
    pallas_call x1, Pallas kernels, outer(): pl.pallas_call(outer_kernel, out_shape=(jax.ShapeDtypeStruct((9, channels...  44.9 us
    pallas_call x1, Pallas kernels, middle(): pl.pallas_call(middle_kernel, out_shape=(jax.ShapeDtypeStruct((pixels, ch...  31.4 us
    pallas_call x1, Pallas kernels, exchange(): pl.pallas_call(lambda *refs: exchange_kernel(count, *refs), out_shape=jax...  10.8 us
    dot_general x6, matrix products, taps_forward(): jnp.einsum('flgi,gio->flgo', shifted, weight[shift_tap], preferred_elemen...  6.38 us
    unnamed x32, local copies, waits for them, and re-layouts  6.25 us
    dot_general x3, matrix products, taps_weight_grad(): jnp.einsum('flgi,flgo->gio', shifted, cotangent, preferred_element_type=j...  4.98 us
    pallas_call x1, Pallas kernels, settle(): pl.pallas_call(settle_kernel, out_shape=jax.ShapeDtypeStruct(values.shape...  4.95 us
    dot_general x3, matrix products, taps_input_grad(): jnp.einsum('flgo,gio->flgi', cotangent, weight[shift_tap], preferred_elem...  4.84 us

profile of v4, /device:TPU:0, one launch (start us, length us, event | category | flops | bytes accessed | tf_op | source)
XLA Modules:
  0.0 135.9 jit_solution(14185420589956268758)
XLA Ops:
  1.3 0.7 convert_bitcast_fusion
  2.0 0.7 fusion.56
  2.7 0.8 select_reduce_fusion.2
  3.6 0.7 multiply_add_fusion
  4.2 0.8 select_reduce_fusion.1
  5.1 0.3 convolution_convert_fusion.1
  5.4 0.7 copy.46
  6.1 10.8 %exchange.1 = bf16[16,32,128]{2,1,0:T(8,128)(2,1)} custom-call(bf16[16,32,128]{2,1,0:T(8,128)(2,1)} %bitcast.150), custom_call_target="tpu_custom_call" | custom-call | tf_op jit(solution)/shard_map/exchange/pallas_call | solution.py:191
  16.9 0.9 slice.86
  17.8 0.8 slice.87
  18.7 0.2 convolution_add_fusion.4
  19.5 0.2 copy.77
  19.7 1.2 fusion.44
  20.9 1.1 convolution_add_fusion.1
  22.1 2.2 %multiply_convert_fusion = (bf16[32,8,8,48]{3,0,1,2:T(8,128)(2,1)S(1)}, f32[32,8,8,48]{3,0,1,2:T(8,128)}) fusion(f32[8,32,8,48]{3,1,2,0:T(8,128)S(1)} %convolution_add_fusion.1, bf16[3,8,16,48]{3,2,1,0:T(8,128)(2,1)} %param.20, bf16[32,8,8,16]{0,3,2,1:T(8,128)(2,1)S(1)} %bitcast.146), kind=kOutput, calls=%fused_computation.26 | convolution fusion | flops 3342336 | bytes 1900544 | tf_op jit(solution)/shard_map/flgi,gio->flgo/dot_general | solution.py:42
  24.3 1.3 fusion.33
  25.6 0.3 convolution_add_fusion.3
  25.9 0.3 fusion.8
  26.2 0.3 copy.52
  26.5 0.4 convert_element_type.105
  27.0 0.2 fusion.26
  27.2 0.4 multiply_reduce_fusion.2
  27.8 1.7 %copy-done.2 = bf16[9,384,384]{2,1,0:T(8,128)(2,1)S(1)} copy-done((bf16[9,384,384]{2,1,0:T(8,128)(2,1)S(1)}, bf16[9,384,384]{2,1,0:T(8,128)(2,1)}, u32[]{:S(2)}) %copy-start.2) | copy-done | bytes 2654232
  29.6 0.9 copy-done.5
  30.5 31.4 %middle.1 = (f32[256,384]{1,0:T(8,128)S(1)}, bf16[256,384]{1,0:T(8,128)(2,1)S(1)}, bf16[16,384,256]{2,1,0:T(8,128)(2,1)S(1)}) custom-call(bf16[256,384]{1,0:T(8,128)(2,1)S(1)} %multiply_convert_fusion.1.act_ref, bf16[256,384]{1,0:T(8,128)(2,1)S(1)} %bitcast.142, bf16[256,384]{1,0:T(8,128)(2,1)S(1)} %bitcast.143, f32[256,1]{1,0:T(8,128)S(1)} %copy.56.weight_ref, ...), custom_call_target="tpu_custom_call" | custom-call | tf_op jit(solution)/shard_map/middle/pallas_call | solution.py:497
  62.0 0.4 multiply_reduce_fusion.1
  62.3 0.5 convolution_convert_fusion
  62.9 1.2 reshape_reshape.3
  64.1 1.7 %convolution_bitcast_fusion.5 = f32[1,8,48,48]{3,2,1,0:T(8,128)S(1)} fusion(bf16[32,8,8,48]{3,0,1,2:T(8,128)(2,1)} %copy-done.11, bf16[32,8,8,48]{3,2,1,0:T(8,128)(2,1)} %reshape_reshape.3), kind=kOutput, calls=%fused_computation.19 | convolution fusion | flops 9437184 | bytes 466944 | tf_op jit(solution)/shard_map/flgi,flgo->gio/dot_general | solution.py:60
  65.8 1.6 %convolution_bitcast_fusion.3 = f32[1,8,48,48]{3,2,1,0:T(8,128)S(1)} fusion(bf16[32,8,8,48]{3,0,1,2:T(8,128)(2,1)} %copy-done.11, bf16[32,8,8,48]{3,2,1,0:T(8,128)(2,1)} %reshape_reshape.3), kind=kOutput, calls=%fused_computation.17 | convolution fusion | flops 7077888 | bytes 991232 | tf_op jit(solution)/shard_map/flgi,flgo->gio/dot_general | solution.py:60
  67.4 1.7 %convolution_bitcast_fusion.4 = f32[1,8,48,48]{3,2,1,0:T(8,128)S(1)} fusion(bf16[32,8,8,48]{3,0,1,2:T(8,128)(2,1)} %copy-done.11, bf16[32,8,8,48]{3,2,1,0:T(8,128)(2,1)} %reshape_reshape.3), kind=kOutput, calls=%fused_computation.18 | convolution fusion | flops 7077888 | bytes 991232 | tf_op jit(solution)/shard_map/flgi,flgo->gio/dot_general | solution.py:60
  69.1 0.9 pad_maximum_fusion
  70.0 1.4 %reshape.197 = f32[432,128]{1,0:T(8,128)S(1)} reshape(f32[3,8,48,48]{3,2,1,0:T(8,128)} %pad_maximum_fusion) | data formatting | bytes 442368 | tf_op jit(solution)/shard_map/reshape | solution.py:801
  71.4 1.6 %convolution_bitcast_fusion = f32[32,8,8,48]{3,0,1,2:T(8,128)S(1)} fusion(bf16[32,8,8,48]{3,2,1,0:T(8,128)(2,1)} %reshape_reshape.3, bf16[3,8,48,48]{3,2,1,0:T(8,128)(2,1)} %param.21), kind=kOutput, calls=%fused_computation | convolution fusion | flops 9437184 | bytes 1015808 | tf_op jit(solution)/shard_map/flgo,gio->flgi/dot_general | solution.py:68
  73.0 1.5 %convolution_bitcast_fusion.2 = f32[32,8,8,48]{3,0,1,2:T(8,128)S(1)} fusion(bf16[32,8,8,48]{3,2,1,0:T(8,128)(2,1)} %reshape_reshape.3, bf16[3,8,48,48]{3,2,1,0:T(8,128)(2,1)} %param.21), kind=kOutput, calls=%fused_computation.2 | convolution fusion | flops 9437184 | bytes 1015808 | tf_op jit(solution)/shard_map/flgo,gio->flgi/dot_general | solution.py:68
  74.6 1.8 %fusion.7 = f32[32,8,8,48]{3,0,1,2:T(8,128)S(1)} fusion(f32[32,8,8,48]{3,0,1,2:T(8,128)S(1)} %copy-done.14, f32[32,6,8,48]{3,0,1,2:T(8,128)S(1)} %slice.93, f32[32,6,8,48]{3,0,1,2:T(8,128)S(1)} %slice.92, bf16[32,8,8,48]{3,2,1,0:T(8,128)(2,1)S(1)} %copy-done.10, bf16[3,8,48,48]{3,2,1,0:T(8,128)(2,1)} %param.21), kind=kOutput, calls=%fused_computation.14 | convolution fusion | flops 10616832 | bytes 4161536 | tf_op jit(solution)/shard_map/flgo,gio->flgi/dot_general | solution.py:68
  76.4 0.7 convolution_bitcast_fusion.6
  77.1 0.7 convolution_bitcast_fusion.8
  77.8 0.7 convolution_bitcast_fusion.7
  78.5 0.7 pad_maximum_fusion.1
  79.2 1.1 reshape.198
  80.3 0.9 copy-done.7
  81.2 44.9 %outer.1 = (f32[9,384,384]{2,1,0:T(8,128)S(1)}, f32[592,128]{1,0:T(8,128)S(1)}) custom-call(bf16[256,384]{1,0:T(8,128)(2,1)S(1)} %copy-done.7, bf16[16,384,256]{2,1,0:T(8,128)(2,1)S(1)} %get-tuple-element.10.gathered_ref, f32[592,128]{1,0:T(8,128)S(1)} %select_maximum_fusion.parts_ref), custom_call_target="tpu_custom_call" | custom-call | tf_op jit(solution)/shard_map/outer/pallas_call | solution.py:664
  126.1 2.3 %copy-done.1 = f32[9,384,384]{2,1,0:T(8,128)} copy-done((f32[9,384,384]{2,1,0:T(8,128)}, f32[9,384,384]{2,1,0:T(8,128)S(1)}, u32[]{:S(2)}) %copy-start.1) | copy-done | bytes 5308440
  128.4 4.9 %settle.1 = f32[9,384,384]{2,1,0:T(8,128)} custom-call(f32[9,384,384]{2,1,0:T(8,128)} %copy-done.1), custom_call_target="tpu_custom_call" | custom-call | tf_op jit(solution)/shard_map/settle/pallas_call | solution.py:700
  133.4 0.6 slice_bitcast_fusion
  134.0 0.8 reshape.201
  134.8 1.1 reshape.202
  (49 shorter events, 1.3 us)
Async XLA Ops:
  0.6 4.5 %copy-start = (bf16[16,8,128]{2,1,0:T(8,128)(2,1)S(1)}, bf16[16,8,128]{2,1,0:T(8,128)(2,1)}, u32[]{:S(2)}) copy-start(bf16[16,8,128]{2,1,0:T(8,128)(2,1)} %param.12) | copy-start | bytes 98308
  19.7 2.4 %copy-start.8 = (bf16[32,8,128]{0,2,1:T(8,128)(2,1)}, bf16[32,8,128]{0,2,1:T(8,128)(2,1)S(1)}, u32[]{:S(2)}) copy-start(bf16[32,8,128]{0,2,1:T(8,128)(2,1)S(1)} %copy.77) | copy-start | bytes 196612
  19.7 5.9 %copy-start.12 = (bf16[3,8,48,48]{3,2,1,0:T(8,128)(2,1)S(1)}, bf16[3,8,48,48]{3,2,1,0:T(8,128)(2,1)}, u32[]{:S(2)}) copy-start(bf16[3,8,48,48]{3,2,1,0:T(8,128)(2,1)} %param.21) | copy-start | bytes 331780
  24.3 3.3 %copy-start.11 = (bf16[32,8,8,48]{3,0,1,2:T(8,128)(2,1)}, bf16[32,8,8,48]{3,0,1,2:T(8,128)(2,1)S(1)}, u32[]{:S(2)}) copy-start(bf16[32,8,8,48]{3,0,1,2:T(8,128)(2,1)S(1)} %get-tuple-element.23) | copy-start | bytes 589828
  24.3 3.0 %copy-start.3 = (bf16[1,256,384]{2,1,0:T(8,128)(2,1)S(1)}, bf16[1,256,384]{2,1,0:T(8,128)(2,1)}, u32[]{:S(2)}) copy-start(bf16[1,256,384]{2,1,0:T(8,128)(2,1)} %param.18) | copy-start | bytes 589828
  24.3 3.0 %copy-start.4 = (bf16[1,256,384]{2,1,0:T(8,128)(2,1)S(1)}, bf16[1,256,384]{2,1,0:T(8,128)(2,1)}, u32[]{:S(2)}) copy-start(bf16[1,256,384]{2,1,0:T(8,128)(2,1)} %param.19) | copy-start | bytes 589828
  24.3 3.4 %copy-start.13 = (f32[384]{0:T(512)S(1)}, f32[384]{0:T(512)}, u32[]{:S(2)}) copy-start(f32[384]{0:T(512)} %param.23) | copy-start | bytes 4612
  27.8 1.8 %copy-start.2 = (bf16[9,384,384]{2,1,0:T(8,128)(2,1)S(1)}, bf16[9,384,384]{2,1,0:T(8,128)(2,1)}, u32[]{:S(2)}) copy-start(bf16[9,384,384]{2,1,0:T(8,128)(2,1)} %kernel_ref.1) | copy-start | bytes 7962628
  29.6 0.9 copy-start.5
  62.0 0.9 copy-start.6
  71.4 3.2 %copy-start.10 = (bf16[32,8,8,48]{3,2,1,0:T(8,128)(2,1)S(1)}, bf16[32,8,8,48]{3,2,1,0:T(8,128)(2,1)}, u32[]{:S(2)}) copy-start(bf16[32,8,8,48]{3,2,1,0:T(8,128)(2,1)} %reshape_reshape.3) | copy-start | bytes 589828
  71.4 3.2 %copy-start.14 = (f32[32,8,8,48]{3,0,1,2:T(8,128)S(1)}, f32[32,8,8,48]{3,0,1,2:T(8,128)}, u32[]{:S(2)}) copy-start(f32[32,8,8,48]{3,0,1,2:T(8,128)} %get-tuple-element.24) | copy-start | bytes 1179652
  73.0 3.4 %copy-start.9 = (bf16[32,8,128]{0,2,1:T(8,128)(2,1)S(1)}, bf16[32,8,128]{0,2,1:T(8,128)(2,1)}, u32[]{:S(2)}) copy-start(bf16[32,8,128]{0,2,1:T(8,128)(2,1)} %copy-done.8) | copy-start | bytes 196612
  80.3 0.9 copy-start.7
  126.1 2.3 %copy-start.1 = (f32[9,384,384]{2,1,0:T(8,128)}, f32[9,384,384]{2,1,0:T(8,128)S(1)}, u32[]{:S(2)}) copy-start(f32[9,384,384]{2,1,0:T(8,128)S(1)} %get-tuple-element.12.x_ref) | copy-start | bytes 15925252

commit v5 on v4

--- a/solution.py
+++ b/solution.py
@@ -688,21 +688,19 @@
     )(grad, gathered, parts)
 
 
-def settle_kernel(x_ref, o_ref, sems):
-    count = x_ref.shape[0]
-    for i in range(count):
-        pltpu.make_async_copy(x_ref.at[i], o_ref.at[i], sems.at[i]).start()
-    for i in range(count):
-        pltpu.make_async_copy(x_ref.at[i], o_ref.at[i], sems.at[i]).wait()
+def settle_kernel(x_ref, o_ref):
+    o_ref[...] = x_ref[...]
 
 
 def settle(values):
+    taps, rows, columns = values.shape
+    block = pl.BlockSpec((1, rows, columns), lambda i: (i, 0, 0))
     return pl.pallas_call(
         settle_kernel,
+        grid=(taps,),
         out_shape=jax.ShapeDtypeStruct(values.shape, values.dtype),
-        in_specs=[pl.BlockSpec(memory_space=VM)],
-        out_specs=pl.BlockSpec(memory_space=pl.ANY),
-        scratch_shapes=[pltpu.SemaphoreType.DMA((values.shape[0],))],
+        in_specs=[block],
+        out_specs=block,
         name="settle",
     )(values)
 

time: 137 us -> 140 us (1.022)
  Pallas kernels: 92 us -> 94.7 us
    pallas_call x1, Pallas kernels: 4.95 us -> 7.6 us  [settle(): pl.pallas_call(settle_kernel, grid=(taps,), out_shape=jax.ShapeDtypeStruc...]
where the time goes in v5:
time: 140 us; the launch traced here: 139 us
  Pallas kernels  94.7 us (68%)
  matrix products  19.5 us (14%)
  local copies, waits for them, and re-layouts  16.1 us (12%)
  other arithmetic  6.52 us (5%)
  between operations  1.68 us (1%)
    pallas_call x1, Pallas kernels, outer(): pl.pallas_call(outer_kernel, out_shape=(jax.ShapeDtypeStruct((9, channels...  44.9 us
    pallas_call x1, Pallas kernels, middle(): pl.pallas_call(middle_kernel, out_shape=(jax.ShapeDtypeStruct((pixels, ch...  31.4 us
    pallas_call x1, Pallas kernels, exchange(): pl.pallas_call(lambda *refs: exchange_kernel(count, *refs), out_shape=jax...  10.8 us
    pallas_call x1, Pallas kernels, settle(): pl.pallas_call(settle_kernel, grid=(taps,), out_shape=jax.ShapeDtypeStruc...  7.6 us
    dot_general x6, matrix products, taps_forward(): jnp.einsum('flgi,gio->flgo', shifted, weight[shift_tap], preferred_elemen...  6.38 us
    unnamed x32, local copies, waits for them, and re-layouts  6.25 us
    dot_general x3, matrix products, taps_weight_grad(): jnp.einsum('flgi,flgo->gio', shifted, cotangent, preferred_element_type=j...  4.98 us
    dot_general x3, matrix products, taps_input_grad(): jnp.einsum('flgo,gio->flgi', cotangent, weight[shift_tap], preferred_elem...  4.84 us

profile of v5, /device:TPU:0, one launch (start us, length us, event | category | flops | bytes accessed | tf_op | source)
XLA Modules:
  0.0 138.5 jit_solution(4788848876230696506)
XLA Ops:
  1.3 0.7 convert_bitcast_fusion
  2.0 0.7 fusion.56
  2.7 0.8 select_reduce_fusion.2
  3.6 0.7 multiply_add_fusion
  4.2 0.8 select_reduce_fusion.1
  5.1 0.3 convolution_convert_fusion.1
  5.4 0.7 copy.46
  6.1 10.8 %exchange.1 = bf16[16,32,128]{2,1,0:T(8,128)(2,1)} custom-call(bf16[16,32,128]{2,1,0:T(8,128)(2,1)} %bitcast.150), custom_call_target="tpu_custom_call" | custom-call | tf_op jit(solution)/shard_map/exchange/pallas_call | solution.py:191
  16.9 0.9 slice.86
  17.8 0.8 slice.87
  18.7 0.2 convolution_add_fusion.4
  19.5 0.2 copy.77
  19.7 1.2 fusion.44
  20.9 1.1 convolution_add_fusion.1
  22.1 2.2 %multiply_convert_fusion = (bf16[32,8,8,48]{3,0,1,2:T(8,128)(2,1)S(1)}, f32[32,8,8,48]{3,0,1,2:T(8,128)}) fusion(f32[8,32,8,48]{3,1,2,0:T(8,128)S(1)} %convolution_add_fusion.1, bf16[3,8,16,48]{3,2,1,0:T(8,128)(2,1)} %param.20, bf16[32,8,8,16]{0,3,2,1:T(8,128)(2,1)S(1)} %bitcast.146), kind=kOutput, calls=%fused_computation.26 | convolution fusion | flops 3342336 | bytes 1900544 | tf_op jit(solution)/shard_map/flgi,gio->flgo/dot_general | solution.py:42
  24.3 1.3 fusion.33
  25.6 0.3 convolution_add_fusion.3
  25.9 0.3 fusion.8
  26.2 0.3 copy.52
  26.5 0.4 convert_element_type.105
  27.0 0.2 fusion.26
  27.2 0.4 multiply_reduce_fusion.2
  27.8 1.7 %copy-done.2 = bf16[9,384,384]{2,1,0:T(8,128)(2,1)S(1)} copy-done((bf16[9,384,384]{2,1,0:T(8,128)(2,1)S(1)}, bf16[9,384,384]{2,1,0:T(8,128)(2,1)}, u32[]{:S(2)}) %copy-start.2) | copy-done | bytes 2654232
  29.6 0.9 copy-done.5
  30.5 31.4 %middle.1 = (f32[256,384]{1,0:T(8,128)S(1)}, bf16[256,384]{1,0:T(8,128)(2,1)S(1)}, bf16[16,384,256]{2,1,0:T(8,128)(2,1)S(1)}) custom-call(bf16[256,384]{1,0:T(8,128)(2,1)S(1)} %multiply_convert_fusion.1.act_ref, bf16[256,384]{1,0:T(8,128)(2,1)S(1)} %bitcast.142, bf16[256,384]{1,0:T(8,128)(2,1)S(1)} %bitcast.143, f32[256,1]{1,0:T(8,128)S(1)} %copy.56.weight_ref, ...), custom_call_target="tpu_custom_call" | custom-call | tf_op jit(solution)/shard_map/middle/pallas_call | solution.py:497
  62.0 0.4 multiply_reduce_fusion.1
  62.3 0.5 convolution_convert_fusion
  62.9 1.2 reshape_reshape.3
  64.1 1.7 %convolution_bitcast_fusion.5 = f32[1,8,48,48]{3,2,1,0:T(8,128)S(1)} fusion(bf16[32,8,8,48]{3,0,1,2:T(8,128)(2,1)} %copy-done.11, bf16[32,8,8,48]{3,2,1,0:T(8,128)(2,1)} %reshape_reshape.3), kind=kOutput, calls=%fused_computation.19 | convolution fusion | flops 9437184 | bytes 466944 | tf_op jit(solution)/shard_map/flgi,flgo->gio/dot_general | solution.py:60
  65.8 1.6 %convolution_bitcast_fusion.3 = f32[1,8,48,48]{3,2,1,0:T(8,128)S(1)} fusion(bf16[32,8,8,48]{3,0,1,2:T(8,128)(2,1)} %copy-done.11, bf16[32,8,8,48]{3,2,1,0:T(8,128)(2,1)} %reshape_reshape.3), kind=kOutput, calls=%fused_computation.17 | convolution fusion | flops 7077888 | bytes 991232 | tf_op jit(solution)/shard_map/flgi,flgo->gio/dot_general | solution.py:60
  67.4 1.7 %convolution_bitcast_fusion.4 = f32[1,8,48,48]{3,2,1,0:T(8,128)S(1)} fusion(bf16[32,8,8,48]{3,0,1,2:T(8,128)(2,1)} %copy-done.11, bf16[32,8,8,48]{3,2,1,0:T(8,128)(2,1)} %reshape_reshape.3), kind=kOutput, calls=%fused_computation.18 | convolution fusion | flops 7077888 | bytes 991232 | tf_op jit(solution)/shard_map/flgi,flgo->gio/dot_general | solution.py:60
  69.1 0.9 pad_maximum_fusion
  70.0 1.4 %reshape.197 = f32[432,128]{1,0:T(8,128)S(1)} reshape(f32[3,8,48,48]{3,2,1,0:T(8,128)} %pad_maximum_fusion) | data formatting | bytes 442368 | tf_op jit(solution)/shard_map/reshape | solution.py:799
  71.4 1.6 %convolution_bitcast_fusion = f32[32,8,8,48]{3,0,1,2:T(8,128)S(1)} fusion(bf16[32,8,8,48]{3,2,1,0:T(8,128)(2,1)} %reshape_reshape.3, bf16[3,8,48,48]{3,2,1,0:T(8,128)(2,1)} %param.21), kind=kOutput, calls=%fused_computation | convolution fusion | flops 9437184 | bytes 1015808 | tf_op jit(solution)/shard_map/flgo,gio->flgi/dot_general | solution.py:68
  73.0 1.5 %convolution_bitcast_fusion.2 = f32[32,8,8,48]{3,0,1,2:T(8,128)S(1)} fusion(bf16[32,8,8,48]{3,2,1,0:T(8,128)(2,1)} %reshape_reshape.3, bf16[3,8,48,48]{3,2,1,0:T(8,128)(2,1)} %param.21), kind=kOutput, calls=%fused_computation.2 | convolution fusion | flops 9437184 | bytes 1015808 | tf_op jit(solution)/shard_map/flgo,gio->flgi/dot_general | solution.py:68
  74.6 1.8 %fusion.7 = f32[32,8,8,48]{3,0,1,2:T(8,128)S(1)} fusion(f32[32,8,8,48]{3,0,1,2:T(8,128)S(1)} %copy-done.14, f32[32,6,8,48]{3,0,1,2:T(8,128)S(1)} %slice.93, f32[32,6,8,48]{3,0,1,2:T(8,128)S(1)} %slice.92, bf16[32,8,8,48]{3,2,1,0:T(8,128)(2,1)S(1)} %copy-done.10, bf16[3,8,48,48]{3,2,1,0:T(8,128)(2,1)} %param.21), kind=kOutput, calls=%fused_computation.14 | convolution fusion | flops 10616832 | bytes 4161536 | tf_op jit(solution)/shard_map/flgo,gio->flgi/dot_general | solution.py:68
  76.4 0.7 convolution_bitcast_fusion.6
  77.1 0.7 convolution_bitcast_fusion.8
  77.8 0.7 convolution_bitcast_fusion.7
  78.5 0.7 pad_maximum_fusion.1
  79.2 1.1 reshape.198
  80.3 0.9 copy-done.7
  81.2 44.9 %outer.1 = (f32[9,384,384]{2,1,0:T(8,128)S(1)}, f32[592,128]{1,0:T(8,128)S(1)}) custom-call(bf16[256,384]{1,0:T(8,128)(2,1)S(1)} %copy-done.7, bf16[16,384,256]{2,1,0:T(8,128)(2,1)S(1)} %get-tuple-element.10.gathered_ref, f32[592,128]{1,0:T(8,128)S(1)} %select_maximum_fusion.parts_ref), custom_call_target="tpu_custom_call" | custom-call | tf_op jit(solution)/shard_map/outer/pallas_call | solution.py:664
  126.1 2.3 %copy-done.1 = f32[9,384,384]{2,1,0:T(8,128)} copy-done((f32[9,384,384]{2,1,0:T(8,128)}, f32[9,384,384]{2,1,0:T(8,128)S(1)}, u32[]{:S(2)}) %copy-start.1) | copy-done | bytes 5308440
  128.4 7.6 %settle.1 = f32[9,384,384]{2,1,0:T(8,128)} custom-call(f32[9,384,384]{2,1,0:T(8,128)} %copy-done.1), custom_call_target="tpu_custom_call" | custom-call | tf_op jit(solution)/shard_map/settle/pallas_call | solution.py:698
  136.0 0.6 slice_bitcast_fusion
  136.7 0.8 reshape.201
  137.5 1.1 reshape.202
  (49 shorter events, 1.3 us)
Async XLA Ops:
  0.6 4.5 %copy-start = (bf16[16,8,128]{2,1,0:T(8,128)(2,1)S(1)}, bf16[16,8,128]{2,1,0:T(8,128)(2,1)}, u32[]{:S(2)}) copy-start(bf16[16,8,128]{2,1,0:T(8,128)(2,1)} %param.12) | copy-start | bytes 98308
  19.7 2.4 %copy-start.8 = (bf16[32,8,128]{0,2,1:T(8,128)(2,1)}, bf16[32,8,128]{0,2,1:T(8,128)(2,1)S(1)}, u32[]{:S(2)}) copy-start(bf16[32,8,128]{0,2,1:T(8,128)(2,1)S(1)} %copy.77) | copy-start | bytes 196612
  19.7 5.9 %copy-start.12 = (bf16[3,8,48,48]{3,2,1,0:T(8,128)(2,1)S(1)}, bf16[3,8,48,48]{3,2,1,0:T(8,128)(2,1)}, u32[]{:S(2)}) copy-start(bf16[3,8,48,48]{3,2,1,0:T(8,128)(2,1)} %param.21) | copy-start | bytes 331780
  24.3 3.3 %copy-start.11 = (bf16[32,8,8,48]{3,0,1,2:T(8,128)(2,1)}, bf16[32,8,8,48]{3,0,1,2:T(8,128)(2,1)S(1)}, u32[]{:S(2)}) copy-start(bf16[32,8,8,48]{3,0,1,2:T(8,128)(2,1)S(1)} %get-tuple-element.23) | copy-start | bytes 589828
  24.3 3.0 %copy-start.3 = (bf16[1,256,384]{2,1,0:T(8,128)(2,1)S(1)}, bf16[1,256,384]{2,1,0:T(8,128)(2,1)}, u32[]{:S(2)}) copy-start(bf16[1,256,384]{2,1,0:T(8,128)(2,1)} %param.18) | copy-start | bytes 589828
  24.3 3.0 %copy-start.4 = (bf16[1,256,384]{2,1,0:T(8,128)(2,1)S(1)}, bf16[1,256,384]{2,1,0:T(8,128)(2,1)}, u32[]{:S(2)}) copy-start(bf16[1,256,384]{2,1,0:T(8,128)(2,1)} %param.19) | copy-start | bytes 589828
  24.3 3.4 %copy-start.13 = (f32[384]{0:T(512)S(1)}, f32[384]{0:T(512)}, u32[]{:S(2)}) copy-start(f32[384]{0:T(512)} %param.23) | copy-start | bytes 4612
  27.8 1.8 %copy-start.2 = (bf16[9,384,384]{2,1,0:T(8,128)(2,1)S(1)}, bf16[9,384,384]{2,1,0:T(8,128)(2,1)}, u32[]{:S(2)}) copy-start(bf16[9,384,384]{2,1,0:T(8,128)(2,1)} %kernel_ref.1) | copy-start | bytes 7962628
  29.6 0.9 copy-start.5
  62.0 0.9 copy-start.6
  71.4 3.2 %copy-start.10 = (bf16[32,8,8,48]{3,2,1,0:T(8,128)(2,1)S(1)}, bf16[32,8,8,48]{3,2,1,0:T(8,128)(2,1)}, u32[]{:S(2)}) copy-start(bf16[32,8,8,48]{3,2,1,0:T(8,128)(2,1)} %reshape_reshape.3) | copy-start | bytes 589828
  71.4 3.2 %copy-start.14 = (f32[32,8,8,48]{3,0,1,2:T(8,128)S(1)}, f32[32,8,8,48]{3,0,1,2:T(8,128)}, u32[]{:S(2)}) copy-start(f32[32,8,8,48]{3,0,1,2:T(8,128)} %get-tuple-element.24) | copy-start | bytes 1179652
  73.0 3.4 %copy-start.9 = (bf16[32,8,128]{0,2,1:T(8,128)(2,1)S(1)}, bf16[32,8,128]{0,2,1:T(8,128)(2,1)}, u32[]{:S(2)}) copy-start(bf16[32,8,128]{0,2,1:T(8,128)(2,1)} %copy-done.8) | copy-start | bytes 196612
  80.3 0.9 copy-start.7
  126.1 2.3 %copy-start.1 = (f32[9,384,384]{2,1,0:T(8,128)}, f32[9,384,384]{2,1,0:T(8,128)S(1)}, u32[]{:S(2)}) copy-start(f32[9,384,384]{2,1,0:T(8,128)S(1)} %get-tuple-element.12.x_ref) | copy-start | bytes 15925252
